TPU v7x, 768 devices: a whole 4x8x12 slice. The times are simulated.
768 devices in a mesh: gx: 16 (over y, core), gy: 12 (over z), gz: 4 (over x).
Axes of the slice: x: 4, y: 8, z: 12, core: 2. Of those that a mesh axis runs over, the one named last changes fastest.
Arguments:
- chi: float32 [256, 192, 512], P('gx', 'gy', 'gz'), may hold values from 0.05 to 4
- inducing: float32 [3, 256, 192, 512], P(None, 'gx', 'gy', 'gz'), may hold values from -6 to 6
- record_dest: int32 [16, 12, 4, 1024, 1], P('gx', 'gy', 'gz'), may hold values from 0 to 3; in each aligned block of 1024 rows (0 to 1023, 1024 to 2047, ..., all dimensions but the last counted through in order) at most 640 rows name the same one
- record_cell: int32 [16, 12, 4, 1024], P('gx', 'gy', 'gz'), may hold values from 0 to 32767
- record_value: float32 [16, 12, 4, 1024], P('gx', 'gy', 'gz'), may hold values from -16 to 16
Outputs:
- potential: float32 [256, 192, 512], P('gx', 'gy', 'gz')
Inputs may be any that keep to these rules, and one draw needn't show every extreme that they name: `record_dest`: among the records of one device, at most 640 go to any one depth brick; in some devices exactly 640 do.
All inputs are finite; a program needn't handle non-finite values.
Results may differ from a plain program's by a relative error of at most 0.0001.
Values sent between devices are 32-bit elements; how exact they have to be, the bound alone decides.
A program may use at most 64 MiB of HBM per device.

v0:
```python
import jax
import jax.numpy as jnp
from jax import lax
from jax.sharding import PartitionSpec as P

SMOOTH = 2
LEVELS = 3
COARSE_SWEEPS = 8
CAP = 640


OMEGA = 0.8


def padded_2(cells, sides, width):
    for axis, dim in sides:
        count = lax.axis_size(axis)
        ends = count - 1
        head = lax.slice_in_dim(cells, 0, width, axis=dim)
        tail = lax.slice_in_dim(cells, cells.shape[dim] - width, cells.shape[dim], axis=dim)
        cells = jnp.concatenate(
            [
                lax.ppermute(tail, axis, [(i, (i + 1) % count) for i in range(ends)]),
                cells,
                lax.ppermute(head, axis, [((i + 1) % count, i) for i in range(ends)]),
            ],
            axis=dim,
        )
    return cells


def restrict(x):
    s = x.shape
    return x.reshape(s[0] // 2, 2, s[1] // 2, 2, s[2] // 2, 2).mean(axis=(1, 3, 5))


def prolong(e):
    return jnp.repeat(jnp.repeat(jnp.repeat(e, 2, 0), 2, 1), 2, 2)


def neighbours(padded):
    return [
        padded[2:, 1:-1, 1:-1],
        padded[:-2, 1:-1, 1:-1],
        padded[1:-1, 2:, 1:-1],
        padded[1:-1, :-2, 1:-1],
        padded[1:-1, 1:-1, 2:],
        padded[1:-1, 1:-1, :-2],
    ]


def moment_pad(x):
    return padded_2(x, (("gx", 0), ("gy", 1), ("gz", 2)), 1)


def fine_pad(x):
    return padded_2(x, (("gx", 0), ("gy", 1), ("gz", 2)), 1)


def middle_pad(x):
    return padded_2(x, (("gx", 0), ("gy", 1), ("gz", 2)), 1)


def coarse_pad(x):
    return padded_2(x, (("gx", 0), ("gy", 1), ("gz", 2)), 1)


def coefficients(kappa, pad_fn):
    return [0.5 * (kappa + other) for other in neighbours(pad_fn(kappa))]


def apply_op(v, coefs, scale, pad_fn):
    total = jnp.zeros_like(v)
    for coef, other in zip(coefs, neighbours(pad_fn(v))):
        total = total + coef * (v - other)
    return scale * total


def relax(rhs, kappa, scale, sweeps, pad_fn):
    coefs = coefficients(kappa, pad_fn)
    diag = scale * (coefs[0] + coefs[1] + coefs[2] + coefs[3] + coefs[4] + coefs[5])
    v = OMEGA * rhs / diag
    for sweep in range(sweeps - 1):
        v = v + OMEGA * (rhs - apply_op(v, coefs, scale, pad_fn)) / diag
    return v


def coarse_solve(rhs, kappa):
    scale = 0.25**LEVELS
    return relax(rhs, kappa, scale, COARSE_SWEEPS, coarse_pad)


def cycle(level, rhs, kappa):
    if level == LEVELS:
        return coarse_solve(rhs, kappa)
    if level < LEVELS - 1:
        pad_fn = fine_pad
    else:
        pad_fn = middle_pad
    scale = 0.25**level
    coefs = coefficients(kappa, pad_fn)
    diag = scale * (coefs[0] + coefs[1] + coefs[2] + coefs[3] + coefs[4] + coefs[5])
    v = OMEGA * rhs / diag
    v = v + OMEGA * (rhs - apply_op(v, coefs, scale, pad_fn)) / diag
    resid = rhs - apply_op(v, coefs, scale, pad_fn)
    corr = cycle(level + 1, restrict(resid), restrict(kappa))
    v = v + prolong(corr)
    for sweep in range(SMOOTH):
        v = v + OMEGA * (rhs - apply_op(v, coefs, scale, pad_fn)) / diag
    return v


def per_device(chi, inducing, record_dest, record_cell, record_value):
    n_gz = lax.axis_size("gz")
    dest = record_dest[0, 0, 0, :, 0]
    cells = record_cell[0, 0, 0]
    values = record_value[0, 0, 0]
    onehot = (dest[:, None] == jnp.arange(n_gz, dtype=jnp.int32)[None, :]).astype(jnp.int32)
    ranks = jnp.sum((jnp.cumsum(onehot, axis=0) - 1) * onehot, axis=1)
    outgoing = jnp.zeros((n_gz, 2, CAP), jnp.float32)
    outgoing = outgoing.at[dest, 0, ranks].set(values)
    outgoing = outgoing.at[dest, 1, ranks].set(cells.astype(jnp.float32))
    incoming = lax.all_to_all(outgoing, "gz", split_axis=0, concat_axis=0, tiled=True)
    in_values = incoming[:, 0].reshape(-1)
    in_cells = incoming[:, 1].reshape(-1).astype(jnp.int32)
    moment_x = moment_pad(chi * inducing[0])
    moment_y = moment_pad(chi * inducing[1])
    moment_z = moment_pad(chi * inducing[2])
    source = -0.5 * (
        moment_x[2:, 1:-1, 1:-1]
        - moment_x[:-2, 1:-1, 1:-1]
        + (moment_y[1:-1, 2:, 1:-1] - moment_y[1:-1, :-2, 1:-1])
        + (moment_z[1:-1, 1:-1, 2:] - moment_z[1:-1, 1:-1, :-2])
    )
    rhs = source.reshape(-1).at[in_cells].add(in_values).reshape(source.shape)
    return cycle(0, rhs, 1.0 + chi)


def solution(mesh):
    placed = (
        P("gx", "gy", "gz"),
        P(None, "gx", "gy", "gz"),
        P("gx", "gy", "gz", None, None),
        P("gx", "gy", "gz", None),
        P("gx", "gy", "gz", None),
    )
    return jax.shard_map(
        per_device, mesh=mesh, in_specs=placed, out_specs=P("gx", "gy", "gz"), check_vma=False
    )
```

profile of v0, /device:TPU:1, one launch (start us, length us, event | category | flops | bytes accessed | tf_op | source)
XLA Modules:
  0.0 656.7 jit_solution(12598122654953994805)
XLA Ops:
  24.5 8.1 %collective-permute-start.12 = (f32[1,16,128]{2,1,0:T(8,128)S(1)}, f32[1,16,128]{2,1,0:T(8,128)S(1)}, u32[]{:S(2)}, u32[]{:S(2)}) collective-permute-start(f32[1,16,128]{2,1,0:T(8,128)S(1)} %get-tuple-element.65), channel_id=1, source_target_pairs={{48,0},{96,48},{144,96},{192,144},{240,192},{288,240},{336,288},{3... | collective-permute-start | bytes 24584 | tf_op jit(solution)/shard_map/ppermute | solution.py:25
  39.0 9.7 %reshape.138 = f32[8,2,8,2,64,2]{5,4,3,2,1,0:T(8,128)} reshape(f32[16,16,128]{2,1,0:T(8,128)S(1)} %get-tuple-element.66) | data formatting | bytes 262144 | tf_op jit(solution)/shard_map/reshape | solution.py:34
  87.3 16.8 %scatter_fusion = f32[32768]{0:T(1024)S(1)} fusion(f32[32768]{0:T(1024)S(1)} %bitcast.43, s32[2560]{0:T(1024)S(1)} %fusion.201, f32[2560]{0:T(1024)S(1)} %reshape.163), kind=kCustom, calls=%fused_computation | custom fusion | flops 2560 | bytes 40960 | tf_op jit(solution)/shard_map/scatter-add | solution.py:135
  104.3 5.0 collective-permute-start.19
  141.1 5.5 collective-permute-start.33
  147.9 5.9 collective-permute-start.27
  170.0 9.7 %reshape.137 = f32[8,2,8,2,64,2]{5,4,3,2,1,0:T(8,128)} reshape(f32[16,16,128]{2,1,0:T(8,128)S(1)} %fusion.45) | data formatting | bytes 262144 | tf_op jit(solution)/shard_map/reshape | solution.py:34
  183.9 5.9 collective-permute-start.37
  214.6 5.1 collective-permute-start.67
  254.9 8.0 %collective-permute-start.55 = (f32[1,4,32]{2,1,0:T(4,128)S(1)}, f32[1,4,32]{2,1,0:T(4,128)S(1)}, u32[]{:S(2)}, u32[]{:S(2)}) collective-permute-start(f32[1,4,32]{2,1,0:T(4,128)S(1)} %get-tuple-element.147), channel_id=1, source_target_pairs={{0,48},{48,96},{96,144},{144,192},{192,240},{240,288},{288,336},{3... | collective-permute-start | bytes 1544 | tf_op jit(solution)/shard_map/ppermute | solution.py:23
  272.8 5.3 collective-permute-start.69
  294.1 5.3 collective-permute-start.63
  314.6 7.0 %collective-permute-start.73 = (f32[1,2,16]{2,1,0:T(2,128)S(1)}, f32[1,2,16]{2,1,0:T(2,128)S(1)}, u32[]{:S(2)}, u32[]{:S(2)}) collective-permute-start(f32[1,2,16]{2,1,0:T(2,128)S(1)} %get-tuple-element.179), channel_id=1, source_target_pairs={{0,48},{48,96},{96,144},{144,192},{192,240},{240,288},{288,336},{3... | collective-permute-start | bytes 392 | tf_op jit(solution)/shard_map/ppermute | solution.py:23
  342.5 5.0 collective-permute-start.79
  369.2 5.2 collective-permute-start.85
  395.5 5.2 collective-permute-start.91
  420.4 5.4 collective-permute-start.97
  444.8 5.4 collective-permute-start.103
  469.8 5.1 collective-permute-start.109
  495.2 5.1 collective-permute-start.115
  520.3 5.4 collective-permute-start.121
  545.4 5.4 collective-permute-start.127
  571.5 5.3 collective-permute-start.133
  598.3 5.3 collective-permute-start.139
  (470 shorter events, 498.9 us)
Async XLA Ops:
  15.6 51.4 %all-to-all-start = ((f32[4,2,640]{2,1,0:T(2,128)}), f32[4,2,640]{2,1,0:T(2,128)S(1)}, u32[]{:S(2)}, u32[]{:S(2)}) async-start(f32[4,2,640]{2,1,0:T(2,128)} %reshape.157), calls=%async_computation | async-start | bytes 40960 | tf_op jit(solution)/shard_map/all_to_all | solution.py:123
  20.5 41.2 %collective-permute-start.13 = (f32[1,16,128]{2,1,0:T(8,128)S(1)}, f32[1,16,128]{2,1,0:T(8,128)S(1)}, u32[]{:S(2)}, u32[]{:S(2)}) collective-permute-start(f32[1,16,128]{2,1,0:T(8,128)S(1)} %get-tuple-element.64), channel_id=1, source_target_pairs={{0,48},{48,96},{96,144},{144,192},{192,240},{240,288},{288,336},{3... | collective-permute-start | bytes 24584 | tf_op jit(solution)/shard_map/ppermute | solution.py:23
  24.5 41.1 %collective-permute-start.12 = (f32[1,16,128]{2,1,0:T(8,128)S(1)}, f32[1,16,128]{2,1,0:T(8,128)S(1)}, u32[]{:S(2)}, u32[]{:S(2)}) collective-permute-start(f32[1,16,128]{2,1,0:T(8,128)S(1)} %get-tuple-element.65), channel_id=1, source_target_pairs={{48,0},{96,48},{144,96},{192,144},{240,192},{288,240},{336,288},{3... | collective-permute-start | bytes 24584 | tf_op jit(solution)/shard_map/ppermute | solution.py:25
  32.7 24.0 %collective-permute-start.6 = (f32[1,16,128]{2,1,0:T(8,128)S(1)}, f32[1,16,128]{2,1,0:T(8,128)S(1)}, u32[]{:S(2)}, u32[]{:S(2)}) collective-permute-start(f32[1,16,128]{2,1,0:T(8,128)S(1)} %get-tuple-element.71), channel_id=1, source_target_pairs={{0,48},{48,96},{96,144},{144,192},{192,240},{240,288},{288,336},{3... | collective-permute-start | bytes 24584 | tf_op jit(solution)/shard_map/ppermute | solution.py:23
  34.6 18.1 %collective-permute-start.2 = (f32[1,16,128]{2,1,0:T(8,128)S(1)}, f32[1,16,128]{2,1,0:T(8,128)S(1)}, u32[]{:S(2)}, u32[]{:S(2)}) collective-permute-start(f32[1,16,128]{2,1,0:T(8,128)S(1)} %get-tuple-element.69), channel_id=1, source_target_pairs={{0,48},{48,96},{96,144},{144,192},{192,240},{240,288},{288,336},{3... | collective-permute-start | bytes 24584 | tf_op jit(solution)/shard_map/ppermute | solution.py:23
  36.5 18.1 %collective-permute-start.3 = (f32[1,16,128]{2,1,0:T(8,128)S(1)}, f32[1,16,128]{2,1,0:T(8,128)S(1)}, u32[]{:S(2)}, u32[]{:S(2)}) collective-permute-start(f32[1,16,128]{2,1,0:T(8,128)S(1)} %get-tuple-element.70), channel_id=1, source_target_pairs={{48,0},{96,48},{144,96},{192,144},{240,192},{288,240},{336,288},{3... | collective-permute-start | bytes 24584 | tf_op jit(solution)/shard_map/ppermute | solution.py:25
  54.7 23.3 %collective-permute-start = (f32[1,16,128]{2,1,0:T(8,128)S(1)}, f32[1,16,128]{2,1,0:T(8,128)S(1)}, u32[]{:S(2)}, u32[]{:S(2)}) collective-permute-start(f32[1,16,128]{2,1,0:T(8,128)S(1)} %get-tuple-element.67), channel_id=1, source_target_pairs={{48,0},{96,48},{144,96},{192,144},{240,192},{288,240},{336,288},{3... | collective-permute-start | bytes 24584 | tf_op jit(solution)/shard_map/ppermute | solution.py:25
  56.7 25.7 %collective-permute-start.1 = (f32[1,16,128]{2,1,0:T(8,128)S(1)}, f32[1,16,128]{2,1,0:T(8,128)S(1)}, u32[]{:S(2)}, u32[]{:S(2)}) collective-permute-start(f32[1,16,128]{2,1,0:T(8,128)S(1)} %get-tuple-element.68), channel_id=1, source_target_pairs={{0,48},{48,96},{96,144},{144,192},{192,240},{240,288},{288,336},{3... | collective-permute-start | bytes 24584 | tf_op jit(solution)/shard_map/ppermute | solution.py:23
  60.3 25.4 %collective-permute-start.4 = (f32[18,1,128]{2,1,0:T(1,128)S(1)}, f32[18,1,128]{2,1,0:T(1,128)S(1)}, u32[]{:S(2)}, u32[]{:S(2)}) collective-permute-start(f32[18,1,128]{2,1,0:T(1,128)S(1)} %get-tuple-element.52), channel_id=1, source_target_pairs={{4,0},{8,4},{12,8},{16,12},{20,16},{24,20},{28,24},{32,28},{36,32}... | collective-permute-start | bytes 27656 | tf_op jit(solution)/shard_map/ppermute | solution.py:25
  72.6 14.4 %collective-permute-start.5 = (f32[18,1,128]{2,1,0:T(1,128)S(1)}, f32[18,1,128]{2,1,0:T(1,128)S(1)}, u32[]{:S(2)}, u32[]{:S(2)}) collective-permute-start(f32[18,1,128]{2,1,0:T(1,128)S(1)} %get-tuple-element.53), channel_id=1, source_target_pairs={{0,4},{4,8},{8,12},{12,16},{16,20},{20,24},{24,28},{28,32},{32,36}... | collective-permute-start | bytes 27656 | tf_op jit(solution)/shard_map/ppermute | solution.py:23
  82.3 21.7 %collective-permute-start.17 = (f32[18,18,1]{2,1,0:T(8,128)S(1)}, f32[18,18,1]{2,1,0:T(8,128)S(1)}, u32[]{:S(2)}, u32[]{:S(2)}) collective-permute-start(f32[18,18,1]{2,1,0:T(8,128)S(1)} %get-tuple-element.38), channel_id=1, source_target_pairs={{0,1},{1,2},{2,3},{4,5},{5,6},{6,7},{8,9},{9,10},{10,11},{12,13},{... | collective-permute-start | bytes 3896 | tf_op jit(solution)/shard_map/ppermute | solution.py:23
  85.7 18.3 %collective-permute-start.16 = (f32[18,18,1]{2,1,0:T(8,128)S(1)}, f32[18,18,1]{2,1,0:T(8,128)S(1)}, u32[]{:S(2)}, u32[]{:S(2)}) collective-permute-start(f32[18,18,1]{2,1,0:T(8,128)S(1)} %get-tuple-element.39), channel_id=1, source_target_pairs={{1,0},{2,1},{3,2},{5,4},{6,5},{7,6},{9,8},{10,9},{11,10},{13,12},{... | collective-permute-start | bytes 3896 | tf_op jit(solution)/shard_map/ppermute | solution.py:25
  117.6 23.5 %collective-permute-start.31 = (f32[1,8,64]{2,1,0:T(8,128)S(1)}, f32[1,8,64]{2,1,0:T(8,128)S(1)}, u32[]{:S(2)}, u32[]{:S(2)}) collective-permute-start(f32[1,8,64]{2,1,0:T(8,128)S(1)} %get-tuple-element.101), channel_id=1, source_target_pairs={{0,48},{48,96},{96,144},{144,192},{192,240},{240,288},{288,336},{3... | collective-permute-start | bytes 6152 | tf_op jit(solution)/shard_map/ppermute | solution.py:23
  119.8 21.3 %collective-permute-start.30 = (f32[1,8,64]{2,1,0:T(8,128)S(1)}, f32[1,8,64]{2,1,0:T(8,128)S(1)}, u32[]{:S(2)}, u32[]{:S(2)}) collective-permute-start(f32[1,8,64]{2,1,0:T(8,128)S(1)} %get-tuple-element.102), channel_id=1, source_target_pairs={{48,0},{96,48},{144,96},{192,144},{240,192},{288,240},{336,288},{3... | collective-permute-start | bytes 6152 | tf_op jit(solution)/shard_map/ppermute | solution.py:25
  135.0 12.9 %collective-permute-start.25 = (f32[1,16,128]{2,1,0:T(8,128)S(1)}, f32[1,16,128]{2,1,0:T(8,128)S(1)}, u32[]{:S(2)}, u32[]{:S(2)}) collective-permute-start(f32[1,16,128]{2,1,0:T(8,128)S(1)} %get-tuple-element.60), channel_id=1, source_target_pairs={{0,48},{48,96},{96,144},{144,192},{192,240},{240,288},{288,336},{3... | collective-permute-start | bytes 24584 | tf_op jit(solution)/shard_map/ppermute | solution.py:23
  141.1 14.1 %collective-permute-start.33 = (f32[10,1,64]{2,1,0:T(1,128)S(1)}, f32[10,1,64]{2,1,0:T(1,128)S(1)}, u32[]{:S(2)}, u32[]{:S(2)}) collective-permute-start(f32[10,1,64]{2,1,0:T(1,128)S(1)} %get-tuple-element.91), channel_id=1, source_target_pairs={{0,4},{4,8},{8,12},{12,16},{16,20},{20,24},{24,28},{28,32},{32,36}... | collective-permute-start | bytes 7688 | tf_op jit(solution)/shard_map/ppermute | solution.py:23
  164.8 18.9 %collective-permute-start.35 = (f32[10,10,1]{2,1,0:T(8,128)S(1)}, f32[10,10,1]{2,1,0:T(8,128)S(1)}, u32[]{:S(2)}, u32[]{:S(2)}) collective-permute-start(f32[10,10,1]{2,1,0:T(8,128)S(1)} %get-tuple-element.81), channel_id=1, source_target_pairs={{0,1},{1,2},{2,3},{4,5},{5,6},{6,7},{8,9},{9,10},{10,11},{12,13},{... | collective-permute-start | bytes 1208 | tf_op jit(solution)/shard_map/ppermute | solution.py:23
  168.2 15.6 %collective-permute-start.34 = (f32[10,10,1]{2,1,0:T(8,128)S(1)}, f32[10,10,1]{2,1,0:T(8,128)S(1)}, u32[]{:S(2)}, u32[]{:S(2)}) collective-permute-start(f32[10,10,1]{2,1,0:T(8,128)S(1)} %get-tuple-element.82), channel_id=1, source_target_pairs={{1,0},{2,1},{3,2},{5,4},{6,5},{7,6},{9,8},{10,9},{11,10},{13,12},{... | collective-permute-start | bytes 1208 | tf_op jit(solution)/shard_map/ppermute | solution.py:25
  183.9 13.7 %collective-permute-start.37 = (f32[1,8,64]{2,1,0:T(8,128)S(1)}, f32[1,8,64]{2,1,0:T(8,128)S(1)}, u32[]{:S(2)}, u32[]{:S(2)}) collective-permute-start(f32[1,8,64]{2,1,0:T(8,128)S(1)} %get-tuple-element.99), channel_id=1, source_target_pairs={{0,48},{48,96},{96,144},{144,192},{192,240},{240,288},{288,336},{3... | collective-permute-start | bytes 6152 | tf_op jit(solution)/shard_map/ppermute | solution.py:23
  191.8 30.4 %collective-permute-start.49 = (f32[1,4,32]{2,1,0:T(4,128)S(1)}, f32[1,4,32]{2,1,0:T(4,128)S(1)}, u32[]{:S(2)}, u32[]{:S(2)}) collective-permute-start(f32[1,4,32]{2,1,0:T(4,128)S(1)} %get-tuple-element.149), channel_id=1, source_target_pairs={{0,48},{48,96},{96,144},{144,192},{192,240},{240,288},{288,336},{3... | collective-permute-start | bytes 1544 | tf_op jit(solution)/shard_map/ppermute | solution.py:23
  195.4 28.7 %collective-permute-start.48 = (f32[1,4,32]{2,1,0:T(4,128)S(1)}, f32[1,4,32]{2,1,0:T(4,128)S(1)}, u32[]{:S(2)}, u32[]{:S(2)}) collective-permute-start(f32[1,4,32]{2,1,0:T(4,128)S(1)} %get-tuple-element.150), channel_id=1, source_target_pairs={{48,0},{96,48},{144,96},{192,144},{240,192},{288,240},{336,288},{3... | collective-permute-start | bytes 1544 | tf_op jit(solution)/shard_map/ppermute | solution.py:25
  212.6 52.2 %collective-permute-start.66 = (f32[1,2,16]{2,1,0:T(2,128)S(1)}, f32[1,2,16]{2,1,0:T(2,128)S(1)}, u32[]{:S(2)}, u32[]{:S(2)}) collective-permute-start(f32[1,2,16]{2,1,0:T(2,128)S(1)} %get-tuple-element.181), channel_id=1, source_target_pairs={{48,0},{96,48},{144,96},{192,144},{240,192},{288,240},{336,288},{3... | collective-permute-start | bytes 392 | tf_op jit(solution)/shard_map/ppermute | solution.py:25
  214.6 50.2 %collective-permute-start.67 = (f32[1,2,16]{2,1,0:T(2,128)S(1)}, f32[1,2,16]{2,1,0:T(2,128)S(1)}, u32[]{:S(2)}, u32[]{:S(2)}) collective-permute-start(f32[1,2,16]{2,1,0:T(2,128)S(1)} %get-tuple-element.182), channel_id=1, source_target_pairs={{0,48},{48,96},{96,144},{144,192},{192,240},{240,288},{288,336},{3... | collective-permute-start | bytes 392 | tf_op jit(solution)/shard_map/ppermute | solution.py:23
  272.8 18.4 %collective-permute-start.69 = (f32[4,1,16]{2,1,0:T(1,128)S(1)}, f32[4,1,16]{2,1,0:T(1,128)S(1)}, u32[]{:S(2)}, u32[]{:S(2)}) collective-permute-start(f32[4,1,16]{2,1,0:T(1,128)S(1)} %get-tuple-element.165), channel_id=1, source_target_pairs={{0,4},{4,8},{8,12},{12,16},{16,20},{20,24},{24,28},{28,32},{32,36}... | collective-permute-start | bytes 776 | tf_op jit(solution)/shard_map/ppermute | solution.py:23
  (129 other events, 852.9 us)
where the time goes:
time: 665 us; the launch traced here: 657 us
  starting transfers between devices  449 us (68%)
  waiting for transfers between devices  133 us (20%)
  other arithmetic  36.3 us (5%)
  local copies, waits for them, and re-layouts  35.1 us (5%)
    ppermute x75, starting transfers between devices, padded_2(): lax.ppermute(tail, axis, [(i, (i + 1) % count) for i in range(ends)])  324 us
    ppermute x75, starting transfers between devices, padded_2(): lax.ppermute(head, axis, [((i + 1) % count, i) for i in range(ends)])  120 us
    ppermute x75, waiting for transfers between devices, padded_2(): lax.ppermute(head, axis, [((i + 1) % count, i) for i in range(ends)])  117 us
    reshape x4, local copies, waits for them, and re-layouts, restrict(): x.reshape(s[0] // 2, 2, s[1] // 2, 2, s[2] // 2, 2).mean(axis=(1, 3, 5))  20.6 us
    scatter-add x1, other arithmetic, per_device(): rhs = source.reshape(-1).at[in_cells].add(in_values).reshape(source.shape)  16.8 us
    ppermute x75, waiting for transfers between devices, padded_2(): lax.ppermute(tail, axis, [(i, (i + 1) % count) for i in range(ends)])  16 us
  transfers between devices with their start and end apart: 151, of which 53 were waited for; matrix products, arithmetic and copies ran while one was open for 8% of the time, Pallas kernels for 0%

commit v1 on v0

v1 whole, which is shorter than its diff:
```python
import functools
import itertools

import jax
import jax.numpy as jnp
from jax import lax
from jax.experimental import pallas as pl
from jax.experimental.pallas import tpu as pltpu
from jax.sharding import PartitionSpec as P

OMEGA = 0.8
F32 = jnp.float32
BF16 = jnp.bfloat16
MESH = pl.DeviceIdType.MESH
BOX = [d for d in itertools.product((-1, 0, 1), repeat=3) if d != (0, 0, 0)]
BOX2 = [d for d in itertools.product((-1, 0, 1), repeat=2) if d != (0, 0)]
REACH = 5


class Level:
    def __init__(self, index, own, size, split, total):
        self.index, self.own, self.size, self.split, self.total = index, own, size, split, total
        self.scale = 0.25**index


L0 = Level(0, (16, 16, 128), (22, 24, 256), (19, 20, 192), (256, 192, 512))
L1 = Level(1, (8, 8, 64), (16, 16, 128), (12, 12, 96), (128, 96, 256))
L2 = Level(2, (4, 4, 0), (12, 16, 128), (8, 8, 128), (64, 48, 128))
L3 = Level(3, (2, 2, 0), (22, 24, 128), (12, 24, 128), (32, 24, 64))
LEVELS = (L0, L1, L2, L3)


def tiles_0(d):
    if d[2] == 0:
        if d[1] == 0:
            return 6
        return 8 if d[0] == 0 else 2
    return 2 if d[1] == 0 else 1


def tiles_1(d):
    if d[2] == 0:
        return 4 if d[0] == 0 else 2
    return 2 if d[0] == 0 else 1


def slots(count_of):
    table, at = {}, 0
    for d in BOX:
        table[d] = (at, count_of(d))
        at += count_of(d)
    return table, at


SLOT_0, TILES_0 = slots(tiles_0)
SLOT_1, TILES_1 = slots(tiles_1)


def peers(shape):
    nx, ny, nz = shape
    out = [tuple(d) for d in BOX]
    out += [(0, 0, k) for k in range(2, nz - 1)]
    out += [(0, k, 0) for k in range(2, ny - 1)]
    out += [(k, 0, 0) for k in range(-REACH, REACH + 1) if abs(k) > 1]
    return out


def split3(x):
    hi = x.astype(BF16)
    rest = x - hi.astype(F32)
    mid = rest.astype(BF16)
    low = (rest - mid.astype(F32)).astype(BF16)
    return hi, mid, low


def right(x, mat):
    parts = [jnp.dot(p, mat, preferred_element_type=F32) for p in split3(x)]
    return parts[0] + parts[1] + parts[2]


def left(mat, x):
    parts = [jnp.dot(mat, p, preferred_element_type=F32) for p in split3(x)]
    return parts[0] + parts[1] + parts[2]


def wrap(at, size):
    return jnp.where(at < 0, at + size, jnp.where(at >= size, at - size, at))


def kernel(shape, chi_ref, ind_ref, dest_ref, cell_ref, val_ref, out_ref, *refs):
    it = iter(refs)
    take = lambda n: [next(it) for _ in range(n)]
    K, B, VA, VB, IW, DW = [], [], [], [], [], []
    C = []
    for _ in LEVELS:
        k, b, va, vb, iw, dw, c = take(7)
        K.append(k), B.append(b), VA.append(va), VB.append(vb), IW.append(iw), DW.append(dw), C.append(c)
    rec, mom_out, mom_in, hot, val_hot, rhs = take(6)
    pack_0, land_0, pack_1, land_1 = take(4)
    pack_2, land_2z, full_2, land_2 = take(4)
    pack_3, land_3y, col_3, land_3x = take(4)
    tall_0, tall_1, tall_2, tall_3, tall_4 = take(5)
    send_sem, recv_sem = take(2)

    me = [lax.axis_index(a) for a in ("gx", "gy", "gz")]

    def device(o):
        return tuple(lax.rem(me[i] + (o[i] + shape[i]), shape[i]) for i in range(3))

    barrier = pltpu.get_barrier_semaphore()
    all_peers = peers(shape)
    for o in all_peers:
        pl.semaphore_signal(barrier, inc=1, device_id=device(o), device_id_type=MESH)

    sub = lax.broadcasted_iota(jnp.int32, (8, 128), 0)
    lane = lax.broadcasted_iota(jnp.int32, (8, 128), 1)
    lane16 = lax.broadcasted_iota(jnp.int32, (16, 128), 1)

    def send(src, dst, o, n):
        pltpu.make_async_remote_copy(
            src_ref=src, dst_ref=dst, send_sem=send_sem.at[n], recv_sem=recv_sem.at[n],
            device_id=device(o), device_id_type=MESH,
        ).start()

    def arrive(ref, n):
        pltpu.make_async_copy(ref, ref, recv_sem.at[n]).wait()

    def sent(ref, n):
        pltpu.make_async_copy(ref, ref, send_sem.at[n]).wait()

    def start_0(src, i, n):
        pack, land = pack_0.at[i], land_0.at[i]
        for p in range(3):
            for t in range(2):
                pack[2 * p + t] = src[13 + p, 8 * t : 8 * t + 8, 0:128]
                pack[6 + 2 * p + t] = src[p, 8 * t : 8 * t + 8, 0:128]
        for k in range(8):
            pack[12 + k] = jnp.where(sub >= 4, src[2 * k, 8:16, 0:128], pltpu.roll(src[2 * k + 1, 8:16, 0:128], 4, 0))
            pack[20 + k] = jnp.where(sub < 4, src[2 * k, 0:8, 0:128], pltpu.roll(src[2 * k + 1, 0:8, 0:128], 4, 0))
        up = jnp.zeros((16, 128), F32)
        down = jnp.zeros((16, 128), F32)
        for x in range(16):
            p = src[x, 0:16, 0:128]
            here = (lane16 >= 4 * x) & (lane16 < 4 * x + 4)
            up = jnp.where(here, pltpu.roll(p, (4 * x + 4) % 128, 1), up)
            down = jnp.where(here, pltpu.roll(p, 4 * x, 1) if x else p, down)
        for t in range(2):
            pack[28 + t] = up[8 * t : 8 * t + 8]
            pack[30 + t] = down[8 * t : 8 * t + 8]
        for d in BOX:
            at, count = SLOT_0[d]
            if d[2] == 0:
                if d[1] == 0:
                    first = 0 if d[0] == 1 else 6
                else:
                    first = (12 if d[1] == 1 else 20) + (6 if d[0] == 1 else 0)
            else:
                first = (28 if d[2] == 1 else 30) + (1 if d[1] == 1 else 0)
            send(pack.at[pl.ds(first, count)], land.at[pl.ds(at, count)], d, n)

    def finish_0(dst, i, n):
        land = land_0.at[i]
        arrive(land, n)
        for xp in range(22):
            sx, px = (0, xp) if xp < 16 else (1, xp - 16) if xp < 19 else (-1, xp - 6)
            at = lambda y, z: SLOT_0[(-sx, -y, -z)][0]
            base = 6 if sx == -1 else 0
            if sx:
                row = px - 13 if sx == -1 else px
                dst[xp, 0:8, 0:128] = land[at(0, 0) + 2 * row]
                dst[xp, 8:16, 0:128] = land[at(0, 0) + 2 * row + 1]
            k = px // 2 - base
            above, below = land[at(1, 0) + k], land[at(-1, 0) + k]
            if px % 2:
                above, below = pltpu.roll(above, 4, 0), pltpu.roll(below, 4, 0)
            dst[xp, 16:24, 0:128] = jnp.where(sub < 4, above, below)
            for t in range(3):
                if t < 2:
                    a, b = land[at(0, 1) + t], land[at(0, -1) + t]
                else:
                    a = jnp.where(sub < 4, land[at(1, 1)], land[at(-1, 1)])
                    b = jnp.where(sub < 4, land[at(1, -1)], land[at(-1, -1)])
                a = pltpu.roll(a, (128 - 4 * px) % 128, 1) if px else a
                b = pltpu.roll(b, 124 - 4 * px, 1)
                dst[xp, 8 * t : 8 * t + 8, 128:256] = jnp.where(lane < 64, a, b)

    def start_1(src, i, n):
        pack, land = pack_1.at[i], land_1.at[i]
        for k in range(4):
            pack[k] = jnp.where(lane < 64, src[2 * k, 0:8, :], pltpu.roll(src[2 * k + 1, 0:8, :], 64, 1))
        for t in range(2):
            up = jnp.zeros((8, 128), F32)
            down = jnp.zeros((8, 128), F32)
            for j in range(4):
                p = src[4 * t + j, 0:8, :]
                here = (lane >= 32 * j) & (lane < 32 * j + 32)
                up = jnp.where(here, pltpu.roll(p, (32 * j + 96) % 128, 1) if j != 1 else p, up)
                down = jnp.where(here, pltpu.roll(p, 32 * j, 1) if j else p, down)
            pack[4 + t] = up
            pack[6 + t] = down
        for d in BOX:
            at, count = SLOT_1[d]
            if d[2] == 0:
                first = 2 if d[0] == 1 else 0
            else:
                first = (4 if d[2] == 1 else 6) + (1 if d[0] == 1 else 0)
            send(pack.at[pl.ds(first, count)], land.at[pl.ds(at, count)], d, n)

    def finish_1(dst, i, n):
        land = land_1.at[i]
        arrive(land, n)
        for xp in range(16):
            sx, px = (0, xp) if xp < 8 else (1, xp - 8) if xp < 12 else (-1, xp - 8)
            half = 1 if sx == -1 else 0

            def piece(y, z):
                at = SLOT_1[(-sx, -y, -z)][0]
                return land[at + px // 2 - 2 * half] if z == 0 else land[at + px // 4 - half]

            for t in range(2):
                if t == 0:
                    a, b = piece(0, 1), piece(0, -1)
                    if sx == 0:
                        m = dst[xp, 0:8, :]
                    else:
                        m = piece(0, 0)
                else:
                    m, a, b = (jnp.where(sub < 4, piece(1, z), piece(-1, z)) for z in (0, 1, -1))
                if px % 2 and not (t == 0 and sx == 0):
                    m = pltpu.roll(m, 64, 1)
                sa, sb = (64 - 32 * (px % 4)) % 128, 96 - 32 * (px % 4)
                a = pltpu.roll(a, sa, 1) if sa else a
                b = pltpu.roll(b, sb, 1) if sb else b
                dst[xp, 8 * t : 8 * t + 8, :] = jnp.where(lane < 64, m, jnp.where(lane < 96, a, b))

    def start_2z(i, n):
        for k in range(1, shape[2]):
            send(pack_2.at[i], land_2z.at[i, k - 1], (0, 0, -k), n)

    def finish_2z(i, n):
        arrive(land_2z.at[i], n)
        whole = pack_2[i]
        for k in range(1, shape[2]):
            whole = whole + land_2z[i, k - 1]
        return whole

    def start_2(whole, i, n):
        full_2[i] = whole
        for j, d in enumerate(BOX2):
            send(full_2.at[i], land_2.at[i, j], (d[0], d[1], 0), n)

    def place_2(dst, block, sx, sy):
        x0 = 0 if sx == 0 else 4 if sx == 1 else 8
        y0 = 0 if sy == 0 else 4 if sy == 1 else 12
        for p in range(4):
            dst[x0 + p, y0 : y0 + 4, :] = block[4 * p : 4 * p + 4, :]

    def finish_2(dst, i, n, own=True):
        arrive(land_2.at[i], n)
        for j, d in enumerate(BOX2):
            place_2(dst, land_2[i, j], -d[0], -d[1])
        if own:
            place_2(dst, full_2[i], 0, 0)

    def start_3y(i, n):
        for k in range(1, shape[1]):
            send(pack_3.at[i], land_3y.at[i, k - 1], (0, -k, 0), n)

    def finish_3y(i, n):
        arrive(land_3y.at[i], n)
        col_3[i, 0:2, :] = pack_3[i]
        for k in range(1, shape[1]):
            col_3[i, 2 * k : 2 * k + 2, :] = land_3y[i, k - 1]

    def x_steps():
        return [k for k in range(-REACH, REACH + 1) if k]

    def start_3x(i, n):
        for j, k in enumerate(x_steps()):
            send(col_3.at[i], land_3x.at[i, j], (-k, 0, 0), n)

    def finish_3x(dst, i, n):
        arrive(land_3x.at[i], n)
        for k in range(-REACH, REACH + 1):
            pair = col_3[i] if k == 0 else land_3x[i, x_steps().index(k)]
            dst[(2 * k) % 22] = pair
            dst[(2 * k + 1) % 22] = pltpu.roll(pair, 64, 1)

    def around(ref, x, size):
        nx = size[0]
        v = ref[x]
        nxt = ref[jnp.where(x == nx - 1, 0, x + 1)]
        prv = ref[jnp.where(x == 0, nx - 1, x - 1)]
        return v, (
            nxt, prv,
            pltpu.roll(v, size[1] - 1, 0), pltpu.roll(v, 1, 0),
            pltpu.roll(v, size[2] - 1, 1), pltpu.roll(v, 1, 1),
        )

    def coefficients(lv):
        i = lv.index
        X, Y, Z = lv.size
        rows = lax.broadcasted_iota(jnp.int32, (Y, Z), 0)
        lanes = lax.broadcasted_iota(jnp.int32, (Y, Z), 1)
        y = wrap(me[1] * lv.own[1] + jnp.where(rows < lv.split[1], rows, rows - Y), lv.total[1])
        z = wrap(me[2] * lv.own[2] + jnp.where(lanes < lv.split[2], lanes, lanes - Z), lv.total[2])
        sides = [
            jnp.where(y == lv.total[1] - 1, 0.0, 1.0), jnp.where(y == 0, 0.0, 1.0),
            jnp.where(z == lv.total[2] - 1, 0.0, 1.0), jnp.where(z == 0, 0.0, 1.0),
        ]

        def body(x, carry):
            at = wrap(me[0] * lv.own[0] + jnp.where(x < lv.split[0], x, x - X), lv.total[0])
            masks = [jnp.where(at == lv.total[0] - 1, 0.0, 1.0), jnp.where(at == 0, 0.0, 1.0)] + sides
            k, near = around(K[i], x, lv.size)
            c = [0.5 * (k + m * o) for m, o in zip(masks, near)]
            total = c[0] + c[1] + c[2] + c[3] + c[4] + c[5]
            total = jnp.where(total > 0.5, total, 1.0)
            inv = OMEGA / total
            for j in range(6):
                C[i][j, x] = c[j] * masks[j] * inv
            IW[i][x] = inv * (1.0 / lv.scale)
            DW[i][x] = total * (lv.scale / OMEGA)
            return carry

        lax.fori_loop(0, X, body, 0)

    def gathered(lv, src, x):
        i = lv.index
        v, near = around(src, x, lv.size)
        acc = B[i][x]
        for j in range(6):
            acc = acc + C[i][j, x] * near[j]
        return v, acc

    def sweep(lv, src, dst, unroll=True):
        def body(x, carry):
            v, acc = gathered(lv, src, x)
            dst[x] = (1.0 - OMEGA) * v + acc
            return carry

        lax.fori_loop(0, lv.size[0], body, 0, unroll=unroll)

    def residual(lv, src, x):
        v, acc = gathered(lv, src, x)
        return (acc - OMEGA * v) * DW[lv.index][x]

    def eye(shape2, fn):
        r = lax.broadcasted_iota(jnp.int32, shape2, 0)
        c = lax.broadcasted_iota(jnp.int32, shape2, 1)
        return fn(r, c)

    def as_mat(cond, value=1.0):
        return jnp.where(cond, value, 0.0).astype(BF16)

    half = lambda a: lax.shift_right_arithmetic(a, 1)
    down_rows_0 = eye((8, 16), lambda r, c: as_mat(half(c) == r))
    down_rows = eye((8, 8), lambda r, c: as_mat((half(c) == r) & (r < 4)))
    down_lanes_0 = eye((128, 128), lambda r, c: as_mat(half(r) == c, 0.125))
    down_lanes_1 = eye((128, 128), lambda r, c: as_mat((half(r) + me[2] * 32 == c) & (r < 64), 0.125))
    down_lanes_2 = [
        eye((128, 128), lambda r, c: as_mat(half(r) + 64 * p == c, 0.125)) for p in range(2)
    ]

    def restrict_0(plane):
        for p in range(8):
            tall_0[16 * p : 16 * p + 16, :] = plane(2 * p) + plane(2 * p + 1)
        tall_0[...] = right(tall_0[...], down_lanes_0)
        return [left(down_rows_0, tall_0[16 * p : 16 * p + 16, :]) for p in range(8)]

    def restrict_1(plane, i):
        for p in range(4):
            tall_1[8 * p : 8 * p + 8, :] = plane(2 * p) + plane(2 * p + 1)
        tall_1[...] = right(tall_1[...], down_lanes_1)
        for p in range(4):
            pack_2[i, 4 * p : 4 * p + 4, :] = left(down_rows, tall_1[8 * p : 8 * p + 8, :])[0:4]

    def restrict_2(plane, i):
        both = right(plane(0) + plane(1), down_lanes_2[0]) + right(plane(2) + plane(3), down_lanes_2[1])
        pack_3[i] = left(down_rows, both)[0:2]

    def prolong(fine, coarse, e_ref, v_ref, tall, lanes_mat, rows_of):
        XF, YF, ZF = fine.size
        XC, YC, ZC = coarse.size
        rows_mat = eye((YF, YC), lambda r, c: as_mat(rows_of(r) == c))
        todo = {}
        for x in range(XF):
            rel = x if x < fine.split[0] else x - XF
            todo.setdefault((rel // 2) % XC, []).append(x)
        planes = sorted(todo)
        for q, p in enumerate(planes):
            tall[YC * q : YC * q + YC, :] = e_ref[p]
        spread = right(tall[...], lanes_mat)
        for q, p in enumerate(planes):
            out = left(rows_mat, spread[YC * q : YC * q + YC])
            for x in todo[p]:
                v_ref[x] = v_ref[x] + out

    pl.semaphore_wait(barrier, len(all_peers))

    rec[0, 0:8, :] = dest_ref[...].astype(F32)
    rec[0, 8:16, :] = cell_ref[...].astype(F32)
    rec[0, 16:24, :] = val_ref[...]
    for k in range(1, shape[2]):
        send(rec.at[0], rec.at[k], (0, 0, -k), 0)

    up = jnp.zeros((16, 128), F32)
    down = jnp.zeros((16, 128), F32)
    for x in range(16):
        mz = chi_ref[x] * ind_ref[2, x]
        up = jnp.where(lane16 == x, pltpu.roll(mz, (x + 1) % 128, 1), up)
        down = jnp.where(lane16 == x, pltpu.roll(mz, x, 1) if x else mz, down)
        my = chi_ref[x] * ind_ref[1, x]
        mom_out[2, x : x + 1, :] = my[15:16]
        mom_out[3, x : x + 1, :] = my[0:1]
    mom_out[0] = chi_ref[15] * ind_ref[0, 15]
    mom_out[1] = chi_ref[0] * ind_ref[0, 0]
    mom_out[4] = up
    mom_out[5] = down
    FACES = [(1, 0, 0), (-1, 0, 0), (0, 1, 0), (0, -1, 0), (0, 0, 1), (0, 0, -1)]
    for j, d in enumerate(FACES):
        send(mom_out.at[j], mom_in.at[j], d, 1)

    for lv in LEVELS:
        i = lv.index
        if i:
            K[i][...] = jnp.zeros(lv.size, F32)
            B[i][...] = jnp.zeros(lv.size, F32)

    def fill(x, carry):
        K[0][x] = jnp.zeros((24, 256), F32)
        B[0][x] = jnp.zeros((24, 256), F32)
        return carry

    lax.fori_loop(0, 22, fill, 0)
    for x in range(16):
        K[0][x, 0:16, 0:128] = 1.0 + chi_ref[x]
    start_0(K[0], 0, 2)
    for p, block in enumerate(restrict_0(lambda x: K[0][x, 0:16, 0:128])):
        K[1][p, 0:8, :] = block
    start_1(K[1], 0, 3)
    restrict_1(lambda x: K[1][x, 0:8, :], 0)
    start_2z(0, 4)

    rows256 = lax.broadcasted_iota(jnp.int32, (256, 128), 0).astype(F32)
    rows128 = lax.broadcasted_iota(jnp.int32, (128, 128), 0).astype(F32)
    mine = me[2].astype(F32)

    def deposit(s):
        to, cell = rec[s, 0:8, :], rec[s, 8:16, :]
        row = jnp.floor(cell * (1.0 / 128.0))
        col = cell - 128.0 * row
        row = jnp.where(to == mine, row, -1.0)
        parts = [p.astype(F32) for p in split3(rec[s, 16:24, :])]
        for j in range(8):
            hot[:, 128 * j : 128 * j + 128] = jnp.where(rows256 == row[j : j + 1], 1.0, 0.0).astype(BF16)
            same = rows128 == col[j : j + 1]
            for q in range(3):
                val_hot[128 * q : 128 * q + 128, 128 * j : 128 * j + 128] = jnp.where(same, parts[q][j : j + 1], 0.0).astype(BF16)
        got = lax.dot_general(hot[...], val_hot[...], (((1,), (1,)), ((), ())), preferred_element_type=F32)
        return got[:, 0:128] + got[:, 128:256] + got[:, 256:384]

    rhs[...] = deposit(0)

    arrive(rec.at[pl.ds(1, 3)], 0)

    def more(s, carry):
        rhs[...] = rhs[...] + deposit(s)
        return carry

    lax.fori_loop(1, shape[2], more, 0)

    finish_0(K[0], 0, 2)
    coefficients(L0)

    arrive(mom_in, 1)
    inside = [
        jnp.where(me[i] == edge, 0.0, 1.0) for i in range(3) for edge in (shape[i] - 1, 0)
    ]
    row16 = lax.broadcasted_iota(jnp.int32, (16, 128), 0)
    for x in range(16):
        xp = chi_ref[x + 1] * ind_ref[0, x + 1] if x < 15 else mom_in[1] * inside[0]
        xm = chi_ref[x - 1] * ind_ref[0, x - 1] if x > 0 else mom_in[0] * inside[1]
        my = chi_ref[x] * ind_ref[1, x]
        yp = jnp.where(row16 == 15, mom_in[3, x : x + 1, :] * inside[2], pltpu.roll(my, 15, 0))
        ym = jnp.where(row16 == 0, mom_in[2, x : x + 1, :] * inside[3], pltpu.roll(my, 1, 0))
        mz = chi_ref[x] * ind_ref[2, x]
        far = pltpu.roll(mom_in[5] * inside[4], 127 - x, 1)
        near = mom_in[4] * inside[5]
        near = pltpu.roll(near, 128 - x, 1) if x else near
        zp = jnp.where(lane16 == 127, far, pltpu.roll(mz, 127, 1))
        zm = jnp.where(lane16 == 0, near, pltpu.roll(mz, 1, 1))
        total = -0.5 * (xp - xm + (yp - ym) + (zp - zm)) + rhs[16 * x : 16 * x + 16, :]
        B[0][x, 0:16, 0:128] = total * IW[0][x, 0:16, 0:128]
    start_0(B[0], 1, 5)

    finish_1(K[1], 0, 3)
    coefficients(L1)
    start_2(finish_2z(0, 4), 0, 6)
    for p in range(4):
        K[2][p, 0:4, :] = full_2[0, 4 * p : 4 * p + 4, :]
    restrict_2(lambda x: K[2][x, 0:8, :], 0)
    start_3y(0, 7)

    finish_0(B[0], 1, 5)
    sweep(L0, B[0], VA[0])

    blocks = restrict_0(lambda x: residual(L0, VA[0], x)[0:16, 0:128])
    for p, block in enumerate(blocks):
        B[1][p, 0:8, :] = block * IW[1][p, 0:8, :]
    start_1(B[1], 1, 8)
    finish_2(K[2], 0, 6)
    coefficients(L2)
    finish_3y(0, 7)
    start_3x(0, 9)

    finish_1(B[1], 1, 8)
    sweep(L1, B[1], VA[1])
    restrict_1(lambda x: residual(L1, VA[1], x)[0:8, :], 1)
    start_2z(1, 10)
    finish_3x(K[3], 0, 9)
    coefficients(L3)

    whole = finish_2z(1, 10)
    for p in range(4):
        B[2][p, 0:4, :] = whole[4 * p : 4 * p + 4, :] * IW[2][p, 0:4, :]
        full_2[1, 4 * p : 4 * p + 4, :] = B[2][p, 0:4, :]
    start_2(full_2[1], 1, 11)
    finish_2(B[2], 1, 11, own=False)
    sweep(L2, B[2], VA[2])
    restrict_2(lambda x: residual(L2, VA[2], x)[0:8, :], 1)
    own_rows = pack_3[1]
    low = IW[3][0, 0:2, :]
    high = pltpu.roll(IW[3][1], 64, 1)[0:2, :]
    pack_3[1] = own_rows * jnp.where(lax.broadcasted_iota(jnp.int32, (2, 128), 1) < 64, low, high)
    start_3y(1, 12)
    for p in range(4):
        full_2[2, 4 * p : 4 * p + 4, :] = VA[2][p, 0:4, :]
    start_2(full_2[2], 2, 13)

    finish_3y(1, 12)
    start_3x(1, 14)
    finish_2(VA[2], 2, 13, own=False)
    finish_3x(B[3], 1, 14)
    sweep(L3, B[3], VA[3])

    def two(_, carry):
        sweep(L3, VA[3], VB[3])
        sweep(L3, VB[3], VA[3])
        return carry

    lax.fori_loop(0, 3, two, 0)

    up_2 = eye((128, 128), lambda r, c: as_mat(r == half(c)))
    prolong(L2, L3, VA[3], VA[2], tall_2, up_2, lambda r: wrap(half(jnp.where(r < 8, r, r - 16)), 24))
    sweep(L2, VA[2], VB[2])
    sweep(L2, VB[2], VA[2])
    up_1 = eye((128, 128), lambda r, c: as_mat(r == wrap(half(jnp.where(c < 96, c, c - 128)) + 32 * me[2], 128)))
    prolong(L1, L2, VA[2], VA[1], tall_3, up_1, lambda r: wrap(half(jnp.where(r < 12, r, r - 16)), 16))
    sweep(L1, VA[1], VB[1])
    sweep(L1, VB[1], VA[1])
    up_0 = eye((128, 256), lambda r, c: as_mat(r == wrap(half(jnp.where(c < 192, c, c - 256)), 128)))
    prolong(L0, L1, VA[1], VA[0], tall_4, up_0, lambda r: wrap(half(jnp.where(r < 20, r, r - 24)), 16))
    sweep(L0, VA[0], VB[0])

    for x in range(16):
        v, acc = gathered(L0, VB[0], x)
        out_ref[x] = ((1.0 - OMEGA) * v + acc)[0:16, 0:128]

    sent(rec.at[pl.ds(1, 3)], 0)
    sent(mom_in, 1)
    for i, n in ((0, 2), (1, 5)):
        sent(land_0.at[i], n)
    for i, n in ((0, 3), (1, 8)):
        sent(land_1.at[i], n)
    for i, n in ((0, 4), (1, 10)):
        sent(land_2z.at[i], n)
    for i, n in ((0, 6), (1, 11), (2, 13)):
        sent(land_2.at[i], n)
    for i, n in ((0, 7), (1, 12)):
        sent(land_3y.at[i], n)
    for i, n in ((0, 9), (1, 14)):
        sent(land_3x.at[i], n)


def scratch(shape):
    out = []
    for lv in LEVELS:
        out += [pltpu.VMEM(lv.size, F32)] * 6 + [pltpu.VMEM((6,) + lv.size, F32)]
    ny, nz = shape[1], shape[2]
    out += [
        pltpu.VMEM((nz, 24, 128), F32), pltpu.VMEM((6, 16, 128), F32), pltpu.VMEM((6, 16, 128), F32),
        pltpu.VMEM((256, 1024), BF16), pltpu.VMEM((384, 1024), BF16), pltpu.VMEM((256, 128), F32),
        pltpu.VMEM((2, 32, 8, 128), F32), pltpu.VMEM((2, TILES_0, 8, 128), F32),
        pltpu.VMEM((2, 8, 8, 128), F32), pltpu.VMEM((2, TILES_1, 8, 128), F32),
        pltpu.VMEM((2, 16, 128), F32), pltpu.VMEM((2, nz - 1, 16, 128), F32),
        pltpu.VMEM((3, 16, 128), F32), pltpu.VMEM((3, 8, 16, 128), F32),
        pltpu.VMEM((2, 2, 128), F32), pltpu.VMEM((2, ny - 1, 2, 128), F32),
        pltpu.VMEM((2, 24, 128), F32), pltpu.VMEM((2, 2 * REACH, 24, 128), F32),
        pltpu.VMEM((128, 128), F32), pltpu.VMEM((32, 128), F32),
        pltpu.VMEM((144, 128), F32), pltpu.VMEM((128, 128), F32),
        pltpu.VMEM((192, 128), F32),
        pltpu.SemaphoreType.DMA((15,)), pltpu.SemaphoreType.DMA((15,)),
    ]
    return out


def per_device(shape, chi, inducing, record_dest, record_cell, record_value):
    vmem = pl.BlockSpec(memory_space=pltpu.VMEM)
    return pl.pallas_call(
        functools.partial(kernel, shape),
        out_shape=jax.ShapeDtypeStruct((16, 16, 128), F32),
        in_specs=[vmem] * 5,
        out_specs=vmem,
        scratch_shapes=scratch(shape),
        compiler_params=pltpu.CompilerParams(
            collective_id=0, has_side_effects=True, vmem_limit_bytes=40 * 1024 * 1024
        ),
        name="cycle",
    )(chi, inducing, record_dest.reshape(8, 128), record_cell.reshape(8, 128), record_value.reshape(8, 128))


def solution(mesh):
    shape = tuple(mesh.shape[a] for a in ("gx", "gy", "gz"))
    placed = (
        P("gx", "gy", "gz"),
        P(None, "gx", "gy", "gz"),
        P("gx", "gy", "gz", None, None),
        P("gx", "gy", "gz", None),
        P("gx", "gy", "gz", None),
    )
    return jax.shard_map(
        functools.partial(per_device, shape), mesh=mesh, in_specs=placed, out_specs=P("gx", "gy", "gz"), check_vma=False
    )
```

time: 665 us -> 66.2 us (0.10); the launches traced: 657 us -> 65.9 us
  starting transfers between devices: 449 us -> 0 us
  waiting for transfers between devices: 133 us -> 0 us
  Pallas kernels: 0 us -> 61.3 us
  other arithmetic: 36.3 us -> 0 us
  local copies, waits for them, and re-layouts: 35.1 us -> 4.62 us
    ppermute x150 -> x0, starting transfers between devices: 444 us -> none  [the longest x75 324 us: padded_2(): lax.ppermute(tail, axis, [(i, (i + 1) % count) for i in range(ends)])]
    ppermute x150 -> x0, waiting for transfers between devices: 133 us -> none  [the longest x75 117 us: padded_2(): lax.ppermute(head, axis, [((i + 1) % count, i) for i in range(ends)])]
    pallas_call x0 -> x1, Pallas kernels: none -> 61.3 us  [per_device(): pl.pallas_call(functools.partial(kernel, shape), out_shape=jax.ShapeDtype...]
    reshape x10 -> x0, local copies, waits for them, and re-layouts: 21.7 us -> none  [the longest x4 20.6 us: restrict(): x.reshape(s[0] // 2, 2, s[1] // 2, 2, s[2] // 2, 2).mean(axis=(1, 3, 5))]
    scatter-add x1 -> x0, other arithmetic: 16.8 us -> none  [per_device(): rhs = source.reshape(-1).at[in_cells].add(in_values).reshape(source.shape)]
    reduce_sum x7 -> x0, other arithmetic: 9.37 us -> none  [the longest x6 8.66 us: restrict(): x.reshape(s[0] // 2, 2, s[1] // 2, 2, s[2] // 2, 2).mean(axis=(1, 3, 5))]
  transfers between devices with their start and end apart: 151 -> 0, of which waited for: 53 -> 0; matrix products, arithmetic and copies ran while one was open for 8% -> 0% of each run, Pallas kernels for 0% -> 0%
where the time goes in v1:
time: 66.2 us; the launch traced here: 65.9 us
  Pallas kernels  61.3 us (93%)
  local copies, waits for them, and re-layouts  4.62 us (7%)
    pallas_call x1, Pallas kernels, per_device(): pl.pallas_call(functools.partial(kernel, shape), out_shape=jax.ShapeDtype...  61.3 us
    unnamed x11, local copies, waits for them, and re-layouts  4.62 us

profile of v1, /device:TPU:1, one launch (start us, length us, event | category | flops | bytes accessed | tf_op | source)
XLA Modules:
  0.0 65.9 jit_solution(9524055200397548534)
XLA Ops:
  0.0 0.0 copy-start.2
  0.0 0.7 %copy-done.2 = s32[1,1,1,1024,1]{3,4,2,1,0:T(1,128)S(1)} copy-done((s32[1,1,1,1024,1]{3,4,2,1,0:T(1,128)S(1)}, s32[1,1,1,1024,1]{3,4,2,1,0:T(1,128)}, u32[]{:S(2)}) %copy-start.2) | copy-done | bytes 4120
  0.7 0.0 copy-start
  0.7 1.0 %copy-done = f32[3,16,16,128]{3,2,1,0:T(8,128)S(1)} copy-done((f32[3,16,16,128]{3,2,1,0:T(8,128)S(1)}, f32[3,16,16,128]{3,2,1,0:T(8,128)}, u32[]{:S(2)}) %copy-start) | copy-done | bytes 393240
  1.7 0.0 copy-start.1
  1.7 0.9 %copy-done.1 = f32[16,16,128]{2,1,0:T(8,128)S(1)} copy-done((f32[16,16,128]{2,1,0:T(8,128)S(1)}, f32[16,16,128]{2,1,0:T(8,128)}, u32[]{:S(2)}) %copy-start.1) | copy-done | bytes 131096
  2.6 0.0 copy-start.3
  2.6 0.7 %copy-done.3 = s32[1,1,1,1024]{3,2,1,0:T(1,128)S(1)} copy-done((s32[1,1,1,1024]{3,2,1,0:T(1,128)S(1)}, s32[1,1,1,1024]{3,2,1,0:T(1,128)}, u32[]{:S(2)}) %copy-start.3) | copy-done | bytes 4120
  3.3 0.0 copy-start.4
  3.3 0.7 %copy-done.4 = f32[1,1,1,1024]{3,2,1,0:T(1,128)S(1)} copy-done((f32[1,1,1,1024]{3,2,1,0:T(1,128)S(1)}, f32[1,1,1,1024]{3,2,1,0:T(1,128)}, u32[]{:S(2)}) %copy-start.4) | copy-done | bytes 4120
  4.0 61.3 %cycle.1 = f32[16,16,128]{2,1,0:T(8,128)S(1)} custom-call(f32[16,16,128]{2,1,0:T(8,128)S(1)} %copy-done.1, f32[3,16,16,128]{3,2,1,0:T(8,128)S(1)} %copy-done, s32[8,128]{1,0:T(8,128)S(1)} %bitcast.3, s32[8,128]{1,0:T(8,128)S(1)} %bitcast.4, f32[8,128]{1,0:T(8,128)S(1)} %bitcast.5), custom_call_target="tpu_custom_call" | custom-call | tf_op jit(solution)/shard_map/cycle/pallas_call | solution.py:610
  65.2 0.7 copy.7
Async XLA Ops:
  0.0 0.7 %copy-start.2 = (s32[1,1,1,1024,1]{3,4,2,1,0:T(1,128)S(1)}, s32[1,1,1,1024,1]{3,4,2,1,0:T(1,128)}, u32[]{:S(2)}) copy-start(s32[1,1,1,1024,1]{3,4,2,1,0:T(1,128)} %param.7) | copy-start | bytes 12292
  0.7 1.0 %copy-start = (f32[3,16,16,128]{3,2,1,0:T(8,128)S(1)}, f32[3,16,16,128]{3,2,1,0:T(8,128)}, u32[]{:S(2)}) copy-start(f32[3,16,16,128]{3,2,1,0:T(8,128)} %ind_ref.1) | copy-start | bytes 1179652
  1.7 0.9 %copy-start.1 = (f32[16,16,128]{2,1,0:T(8,128)S(1)}, f32[16,16,128]{2,1,0:T(8,128)}, u32[]{:S(2)}) copy-start(f32[16,16,128]{2,1,0:T(8,128)} %chi_ref.1) | copy-start | bytes 393220
  2.6 0.7 %copy-start.3 = (s32[1,1,1,1024]{3,2,1,0:T(1,128)S(1)}, s32[1,1,1,1024]{3,2,1,0:T(1,128)}, u32[]{:S(2)}) copy-start(s32[1,1,1,1024]{3,2,1,0:T(1,128)} %param.8) | copy-start | bytes 12292
  3.3 0.7 %copy-start.4 = (f32[1,1,1,1024]{3,2,1,0:T(1,128)S(1)}, f32[1,1,1,1024]{3,2,1,0:T(1,128)}, u32[]{:S(2)}) copy-start(f32[1,1,1,1024]{3,2,1,0:T(1,128)} %param.9) | copy-start | bytes 12292

commit v2 on v1

--- a/solution.py
+++ b/solution.py
@@ -13,6 +13,7 @@
 BF16 = jnp.bfloat16
 MESH = pl.DeviceIdType.MESH
 BOX = [d for d in itertools.product((-1, 0, 1), repeat=3) if d != (0, 0, 0)]
+BOX.sort(key=lambda d: -sum(map(abs, d)))
 BOX2 = [d for d in itertools.product((-1, 0, 1), repeat=2) if d != (0, 0)]
 REACH = 5
 
@@ -60,7 +61,7 @@
     nx, ny, nz = shape
     out = [tuple(d) for d in BOX]
     out += [(0, 0, k) for k in range(2, nz - 1)]
-    out += [(0, k, 0) for k in range(2, ny - 1)]
+    out += [(0, k, 0) for k in range(-REACH, REACH + 1) if abs(k) > 1]
     out += [(k, 0, 0) for k in range(-REACH, REACH + 1) if abs(k) > 1]
     return out
 
@@ -87,7 +88,7 @@
     return jnp.where(at < 0, at + size, jnp.where(at >= size, at - size, at))
 
 
-def kernel(shape, chi_ref, ind_ref, dest_ref, cell_ref, val_ref, out_ref, *refs):
+def kernel(shape, chi_hbm, ind_hbm, dest_hbm, cell_hbm, val_hbm, out_ref, *refs):
     it = iter(refs)
     take = lambda n: [next(it) for _ in range(n)]
     K, B, VA, VB, IW, DW = [], [], [], [], [], []
@@ -100,7 +101,8 @@
     pack_2, land_2z, full_2, land_2 = take(4)
     pack_3, land_3y, col_3, land_3x = take(4)
     tall_0, tall_1, tall_2, tall_3, tall_4 = take(5)
-    send_sem, recv_sem = take(2)
+    chi, ind, rec_in, val_in = take(4)
+    send_sem, recv_sem, load_sem = take(3)
 
     me = [lax.axis_index(a) for a in ("gx", "gy", "gz")]
 
@@ -111,6 +113,15 @@
     all_peers = peers(shape)
     for o in all_peers:
         pl.semaphore_signal(barrier, inc=1, device_id=device(o), device_id_type=MESH)
+
+    copies = [
+        pltpu.make_async_copy(src, dst, load_sem.at[j])
+        for j, (src, dst) in enumerate([
+            (chi_hbm, chi), (ind_hbm, ind), (dest_hbm, rec_in.at[0]), (cell_hbm, rec_in.at[1]), (val_hbm, val_in),
+        ])
+    ]
+    for j in (2, 3, 4, 0, 1):
+        copies[j].start()
 
     sub = lax.broadcasted_iota(jnp.int32, (8, 128), 0)
     lane = lax.broadcasted_iota(jnp.int32, (8, 128), 1)
@@ -128,8 +139,8 @@
     def sent(ref, n):
         pltpu.make_async_copy(ref, ref, send_sem.at[n]).wait()
 
-    def start_0(src, i, n):
-        pack, land = pack_0.at[i], land_0.at[i]
+    def make_0(src, i):
+        pack = pack_0.at[i]
         for p in range(3):
             for t in range(2):
                 pack[2 * p + t] = src[13 + p, 8 * t : 8 * t + 8, 0:128]
@@ -147,6 +158,9 @@
         for t in range(2):
             pack[28 + t] = up[8 * t : 8 * t + 8]
             pack[30 + t] = down[8 * t : 8 * t + 8]
+
+    def ship_0(i, n):
+        pack, land = pack_0.at[i], land_0.at[i]
         for d in BOX:
             at, count = SLOT_0[d]
             if d[2] == 0:
@@ -234,7 +248,7 @@
                 dst[xp, 8 * t : 8 * t + 8, :] = jnp.where(lane < 64, m, jnp.where(lane < 96, a, b))
 
     def start_2z(i, n):
-        for k in range(1, shape[2]):
+        for k in (2, 1, 3):
             send(pack_2.at[i], land_2z.at[i, k - 1], (0, 0, -k), n)
 
     def finish_2z(i, n):
@@ -262,43 +276,44 @@
         if own:
             place_2(dst, full_2[i], 0, 0)
 
+    steps = sorted([k for k in range(-REACH, REACH + 1) if k], key=lambda k: -abs(k))
+
     def start_3y(i, n):
-        for k in range(1, shape[1]):
-            send(pack_3.at[i], land_3y.at[i, k - 1], (0, -k, 0), n)
+        for j, k in enumerate(steps):
+            send(pack_3.at[i], land_3y.at[i, j], (0, -k, 0), n)
 
     def finish_3y(i, n):
         arrive(land_3y.at[i], n)
+        col_3[i, 2 * REACH + 2 : 24 - 2 * REACH, :] = jnp.zeros((22 - 4 * REACH, 128), F32)
         col_3[i, 0:2, :] = pack_3[i]
-        for k in range(1, shape[1]):
-            col_3[i, 2 * k : 2 * k + 2, :] = land_3y[i, k - 1]
-
-    def x_steps():
-        return [k for k in range(-REACH, REACH + 1) if k]
+        for j, k in enumerate(steps):
+            row = (2 * k) % 24
+            col_3[i, row : row + 2, :] = land_3y[i, j]
 
     def start_3x(i, n):
-        for j, k in enumerate(x_steps()):
+        for j, k in enumerate(steps):
             send(col_3.at[i], land_3x.at[i, j], (-k, 0, 0), n)
 
     def finish_3x(dst, i, n):
         arrive(land_3x.at[i], n)
         for k in range(-REACH, REACH + 1):
-            pair = col_3[i] if k == 0 else land_3x[i, x_steps().index(k)]
+            pair = col_3[i] if k == 0 else land_3x[i, steps.index(k)]
             dst[(2 * k) % 22] = pair
             dst[(2 * k + 1) % 22] = pltpu.roll(pair, 64, 1)
 
     def around(ref, x, size):
         nx = size[0]
         v = ref[x]
-        nxt = ref[jnp.where(x == nx - 1, 0, x + 1)]
-        prv = ref[jnp.where(x == 0, nx - 1, x - 1)]
         return v, (
-            nxt, prv,
+            ref[(x + 1) % nx], ref[(x - 1) % nx],
             pltpu.roll(v, size[1] - 1, 0), pltpu.roll(v, 1, 0),
             pltpu.roll(v, size[2] - 1, 1), pltpu.roll(v, 1, 1),
         )
 
-    def coefficients(lv):
-        i = lv.index
+    def planes(lv, halo):
+        return [r % lv.size[0] for r in range(-halo, lv.own[0] + halo)]
+
+    def edge_masks(lv):
         X, Y, Z = lv.size
         rows = lax.broadcasted_iota(jnp.int32, (Y, Z), 0)
         lanes = lax.broadcasted_iota(jnp.int32, (Y, Z), 1)
@@ -309,21 +324,31 @@
             jnp.where(z == lv.total[2] - 1, 0.0, 1.0), jnp.where(z == 0, 0.0, 1.0),
         ]
 
-        def body(x, carry):
-            at = wrap(me[0] * lv.own[0] + jnp.where(x < lv.split[0], x, x - X), lv.total[0])
-            masks = [jnp.where(at == lv.total[0] - 1, 0.0, 1.0), jnp.where(at == 0, 0.0, 1.0)] + sides
-            k, near = around(K[i], x, lv.size)
-            c = [0.5 * (k + m * o) for m, o in zip(masks, near)]
-            total = c[0] + c[1] + c[2] + c[3] + c[4] + c[5]
-            total = jnp.where(total > 0.5, total, 1.0)
+        def at(x):
+            rel = x if x < lv.split[0] else x - X
+            g = wrap(me[0] * lv.own[0] + rel, lv.total[0])
+            return [jnp.where(g == lv.total[0] - 1, 0.0, 1.0), jnp.where(g == 0, 0.0, 1.0)] + sides
+
+        return at
+
+    def face_sums(lv, x, masks):
+        k, near = around(K[lv.index], x, lv.size)
+        c = [0.5 * (k + m * o) for m, o in zip(masks, near)]
+        total = c[0] + c[1] + c[2] + c[3] + c[4] + c[5]
+        return c, jnp.where(total > 0.5, total, 1.0)
+
+    def coefficients(lv, halo):
+        i = lv.index
+        at = edge_masks(lv)
+        for x in planes(lv, halo):
+            masks = at(x)
+            c, total = face_sums(lv, x, masks)
             inv = OMEGA / total
             for j in range(6):
                 C[i][j, x] = c[j] * masks[j] * inv
-            IW[i][x] = inv * (1.0 / lv.scale)
-            DW[i][x] = total * (lv.scale / OMEGA)
-            return carry
-
-        lax.fori_loop(0, X, body, 0)
+            if x < lv.own[0]:
+                IW[i][x] = inv * (1.0 / lv.scale)
+                DW[i][x] = total * (lv.scale / OMEGA)
 
     def gathered(lv, src, x):
         i = lv.index
@@ -333,13 +358,10 @@
             acc = acc + C[i][j, x] * near[j]
         return v, acc
 
-    def sweep(lv, src, dst, unroll=True):
-        def body(x, carry):
+    def sweep(lv, src, dst, halo):
+        for x in planes(lv, halo):
             v, acc = gathered(lv, src, x)
             dst[x] = (1.0 - OMEGA) * v + acc
-            return carry
-
-        lax.fori_loop(0, lv.size[0], body, 0, unroll=unroll)
 
     def residual(lv, src, x):
         v, acc = gathered(lv, src, x)
@@ -379,63 +401,57 @@
         both = right(plane(0) + plane(1), down_lanes_2[0]) + right(plane(2) + plane(3), down_lanes_2[1])
         pack_3[i] = left(down_rows, both)[0:2]
 
-    def prolong(fine, coarse, e_ref, v_ref, tall, lanes_mat, rows_of):
+    def prolong(fine, coarse, halo, e_ref, v_ref, tall, lanes_mat, rows_of):
         XF, YF, ZF = fine.size
         XC, YC, ZC = coarse.size
         rows_mat = eye((YF, YC), lambda r, c: as_mat(rows_of(r) == c))
         todo = {}
-        for x in range(XF):
-            rel = x if x < fine.split[0] else x - XF
-            todo.setdefault((rel // 2) % XC, []).append(x)
-        planes = sorted(todo)
-        for q, p in enumerate(planes):
+        for rel in range(-halo, fine.own[0] + halo):
+            todo.setdefault((rel // 2) % XC, []).append(rel % XF)
+        for q, p in enumerate(todo):
             tall[YC * q : YC * q + YC, :] = e_ref[p]
         spread = right(tall[...], lanes_mat)
-        for q, p in enumerate(planes):
+        for q, p in enumerate(todo):
             out = left(rows_mat, spread[YC * q : YC * q + YC])
             for x in todo[p]:
                 v_ref[x] = v_ref[x] + out
 
-    pl.semaphore_wait(barrier, len(all_peers))
-
-    rec[0, 0:8, :] = dest_ref[...].astype(F32)
-    rec[0, 8:16, :] = cell_ref[...].astype(F32)
-    rec[0, 16:24, :] = val_ref[...]
-    for k in range(1, shape[2]):
-        send(rec.at[0], rec.at[k], (0, 0, -k), 0)
-
+    for copy in copies[2:]:
+        copy.wait()
+    rec[0, 0:8, :] = rec_in[0].astype(F32)
+    rec[0, 8:16, :] = rec_in[1].astype(F32)
+    rec[0, 16:24, :] = val_in[...]
+    copies[0].wait()
+    for x in range(16):
+        K[0][x, 0:16, 0:128] = 1.0 + chi[x]
+    make_0(K[0], 0)
+    copies[1].wait()
     up = jnp.zeros((16, 128), F32)
     down = jnp.zeros((16, 128), F32)
     for x in range(16):
-        mz = chi_ref[x] * ind_ref[2, x]
+        mz = chi[x] * ind[2, x]
         up = jnp.where(lane16 == x, pltpu.roll(mz, (x + 1) % 128, 1), up)
         down = jnp.where(lane16 == x, pltpu.roll(mz, x, 1) if x else mz, down)
-        my = chi_ref[x] * ind_ref[1, x]
+        my = chi[x] * ind[1, x]
         mom_out[2, x : x + 1, :] = my[15:16]
         mom_out[3, x : x + 1, :] = my[0:1]
-    mom_out[0] = chi_ref[15] * ind_ref[0, 15]
-    mom_out[1] = chi_ref[0] * ind_ref[0, 0]
+    mom_out[0] = chi[15] * ind[0, 15]
+    mom_out[1] = chi[0] * ind[0, 0]
     mom_out[4] = up
     mom_out[5] = down
+
+    pl.semaphore_wait(barrier, len(all_peers))
+
+    for k in (2, 1, 3):
+        send(rec.at[0], rec.at[k], (0, 0, -k), 0)
     FACES = [(1, 0, 0), (-1, 0, 0), (0, 1, 0), (0, -1, 0), (0, 0, 1), (0, 0, -1)]
     for j, d in enumerate(FACES):
         send(mom_out.at[j], mom_in.at[j], d, 1)
-
-    for lv in LEVELS:
-        i = lv.index
-        if i:
-            K[i][...] = jnp.zeros(lv.size, F32)
-            B[i][...] = jnp.zeros(lv.size, F32)
-
-    def fill(x, carry):
-        K[0][x] = jnp.zeros((24, 256), F32)
-        B[0][x] = jnp.zeros((24, 256), F32)
-        return carry
-
-    lax.fori_loop(0, 22, fill, 0)
-    for x in range(16):
-        K[0][x, 0:16, 0:128] = 1.0 + chi_ref[x]
-    start_0(K[0], 0, 2)
+    ship_0(0, 2)
+
+    for ref in (K[2], B[2]):
+        for x in range(12):
+            ref[x, 8:16, :] = jnp.zeros((8, 128), F32)
     for p, block in enumerate(restrict_0(lambda x: K[0][x, 0:16, 0:128])):
         K[1][p, 0:8, :] = block
     start_1(K[1], 0, 3)
@@ -471,31 +487,34 @@
     lax.fori_loop(1, shape[2], more, 0)
 
     finish_0(K[0], 0, 2)
-    coefficients(L0)
 
     arrive(mom_in, 1)
     inside = [
         jnp.where(me[i] == edge, 0.0, 1.0) for i in range(3) for edge in (shape[i] - 1, 0)
     ]
+    masks_0 = edge_masks(L0)
     row16 = lax.broadcasted_iota(jnp.int32, (16, 128), 0)
     for x in range(16):
-        xp = chi_ref[x + 1] * ind_ref[0, x + 1] if x < 15 else mom_in[1] * inside[0]
-        xm = chi_ref[x - 1] * ind_ref[0, x - 1] if x > 0 else mom_in[0] * inside[1]
-        my = chi_ref[x] * ind_ref[1, x]
+        xp = chi[x + 1] * ind[0, x + 1] if x < 15 else mom_in[1] * inside[0]
+        xm = chi[x - 1] * ind[0, x - 1] if x > 0 else mom_in[0] * inside[1]
+        my = chi[x] * ind[1, x]
         yp = jnp.where(row16 == 15, mom_in[3, x : x + 1, :] * inside[2], pltpu.roll(my, 15, 0))
         ym = jnp.where(row16 == 0, mom_in[2, x : x + 1, :] * inside[3], pltpu.roll(my, 1, 0))
-        mz = chi_ref[x] * ind_ref[2, x]
+        mz = chi[x] * ind[2, x]
         far = pltpu.roll(mom_in[5] * inside[4], 127 - x, 1)
         near = mom_in[4] * inside[5]
         near = pltpu.roll(near, 128 - x, 1) if x else near
         zp = jnp.where(lane16 == 127, far, pltpu.roll(mz, 127, 1))
         zm = jnp.where(lane16 == 0, near, pltpu.roll(mz, 1, 1))
         total = -0.5 * (xp - xm + (yp - ym) + (zp - zm)) + rhs[16 * x : 16 * x + 16, :]
-        B[0][x, 0:16, 0:128] = total * IW[0][x, 0:16, 0:128]
-    start_0(B[0], 1, 5)
+        sums = face_sums(L0, x, masks_0(x))[1][0:16, 0:128]
+        B[0][x, 0:16, 0:128] = total * (OMEGA / sums)
+    make_0(B[0], 1)
+    ship_0(1, 5)
+    coefficients(L0, 2)
 
     finish_1(K[1], 0, 3)
-    coefficients(L1)
+    coefficients(L1, 3)
     start_2(finish_2z(0, 4), 0, 6)
     for p in range(4):
         K[2][p, 0:4, :] = full_2[0, 4 * p : 4 * p + 4, :]
@@ -503,23 +522,23 @@
     start_3y(0, 7)
 
     finish_0(B[0], 1, 5)
-    sweep(L0, B[0], VA[0])
+    sweep(L0, B[0], VA[0], 2)
 
     blocks = restrict_0(lambda x: residual(L0, VA[0], x)[0:16, 0:128])
     for p, block in enumerate(blocks):
         B[1][p, 0:8, :] = block * IW[1][p, 0:8, :]
     start_1(B[1], 1, 8)
     finish_2(K[2], 0, 6)
-    coefficients(L2)
+    coefficients(L2, 3)
     finish_3y(0, 7)
     start_3x(0, 9)
 
     finish_1(B[1], 1, 8)
-    sweep(L1, B[1], VA[1])
+    sweep(L1, B[1], VA[1], 3)
     restrict_1(lambda x: residual(L1, VA[1], x)[0:8, :], 1)
     start_2z(1, 10)
     finish_3x(K[3], 0, 9)
-    coefficients(L3)
+    coefficients(L3, 8)
 
     whole = finish_2z(1, 10)
     for p in range(4):
@@ -527,7 +546,7 @@
         full_2[1, 4 * p : 4 * p + 4, :] = B[2][p, 0:4, :]
     start_2(full_2[1], 1, 11)
     finish_2(B[2], 1, 11, own=False)
-    sweep(L2, B[2], VA[2])
+    sweep(L2, B[2], VA[2], 3)
     restrict_2(lambda x: residual(L2, VA[2], x)[0:8, :], 1)
     own_rows = pack_3[1]
     low = IW[3][0, 0:2, :]
@@ -542,26 +561,22 @@
     start_3x(1, 14)
     finish_2(VA[2], 2, 13, own=False)
     finish_3x(B[3], 1, 14)
-    sweep(L3, B[3], VA[3])
-
-    def two(_, carry):
-        sweep(L3, VA[3], VB[3])
-        sweep(L3, VB[3], VA[3])
-        return carry
-
-    lax.fori_loop(0, 3, two, 0)
+    now, other = B[3], VA[3]
+    for halo in range(8, 1, -1):
+        sweep(L3, now, other, halo)
+        now, other = other, VB[3] if other is VA[3] else VA[3]
 
     up_2 = eye((128, 128), lambda r, c: as_mat(r == half(c)))
-    prolong(L2, L3, VA[3], VA[2], tall_2, up_2, lambda r: wrap(half(jnp.where(r < 8, r, r - 16)), 24))
-    sweep(L2, VA[2], VB[2])
-    sweep(L2, VB[2], VA[2])
+    prolong(L2, L3, 4, now, VA[2], tall_2, up_2, lambda r: wrap(half(jnp.where(r < 8, r, r - 16)), 24))
+    sweep(L2, VA[2], VB[2], 3)
+    sweep(L2, VB[2], VA[2], 2)
     up_1 = eye((128, 128), lambda r, c: as_mat(r == wrap(half(jnp.where(c < 96, c, c - 128)) + 32 * me[2], 128)))
-    prolong(L1, L2, VA[2], VA[1], tall_3, up_1, lambda r: wrap(half(jnp.where(r < 12, r, r - 16)), 16))
-    sweep(L1, VA[1], VB[1])
-    sweep(L1, VB[1], VA[1])
+    prolong(L1, L2, 3, VA[2], VA[1], tall_3, up_1, lambda r: wrap(half(jnp.where(r < 12, r, r - 16)), 16))
+    sweep(L1, VA[1], VB[1], 2)
+    sweep(L1, VB[1], VA[1], 1)
     up_0 = eye((128, 256), lambda r, c: as_mat(r == wrap(half(jnp.where(c < 192, c, c - 256)), 128)))
-    prolong(L0, L1, VA[1], VA[0], tall_4, up_0, lambda r: wrap(half(jnp.where(r < 20, r, r - 24)), 16))
-    sweep(L0, VA[0], VB[0])
+    prolong(L0, L1, 2, VA[1], VA[0], tall_4, up_0, lambda r: wrap(half(jnp.where(r < 20, r, r - 24)), 16))
+    sweep(L0, VA[0], VB[0], 1)
 
     for x in range(16):
         v, acc = gathered(L0, VB[0], x)
@@ -587,7 +602,7 @@
     out = []
     for lv in LEVELS:
         out += [pltpu.VMEM(lv.size, F32)] * 6 + [pltpu.VMEM((6,) + lv.size, F32)]
-    ny, nz = shape[1], shape[2]
+    nz = shape[2]
     out += [
         pltpu.VMEM((nz, 24, 128), F32), pltpu.VMEM((6, 16, 128), F32), pltpu.VMEM((6, 16, 128), F32),
         pltpu.VMEM((256, 1024), BF16), pltpu.VMEM((384, 1024), BF16), pltpu.VMEM((256, 128), F32),
@@ -595,12 +610,14 @@
         pltpu.VMEM((2, 8, 8, 128), F32), pltpu.VMEM((2, TILES_1, 8, 128), F32),
         pltpu.VMEM((2, 16, 128), F32), pltpu.VMEM((2, nz - 1, 16, 128), F32),
         pltpu.VMEM((3, 16, 128), F32), pltpu.VMEM((3, 8, 16, 128), F32),
-        pltpu.VMEM((2, 2, 128), F32), pltpu.VMEM((2, ny - 1, 2, 128), F32),
+        pltpu.VMEM((2, 2, 128), F32), pltpu.VMEM((2, 2 * REACH, 2, 128), F32),
         pltpu.VMEM((2, 24, 128), F32), pltpu.VMEM((2, 2 * REACH, 24, 128), F32),
         pltpu.VMEM((128, 128), F32), pltpu.VMEM((32, 128), F32),
         pltpu.VMEM((144, 128), F32), pltpu.VMEM((128, 128), F32),
-        pltpu.VMEM((192, 128), F32),
-        pltpu.SemaphoreType.DMA((15,)), pltpu.SemaphoreType.DMA((15,)),
+        pltpu.VMEM((160, 128), F32),
+        pltpu.VMEM((16, 16, 128), F32), pltpu.VMEM((3, 16, 16, 128), F32),
+        pltpu.VMEM((2, 8, 128), jnp.int32), pltpu.VMEM((8, 128), F32),
+        pltpu.SemaphoreType.DMA((15,)), pltpu.SemaphoreType.DMA((15,)), pltpu.SemaphoreType.DMA((5,)),
     ]
     return out
 
@@ -610,7 +627,7 @@
     return pl.pallas_call(
         functools.partial(kernel, shape),
         out_shape=jax.ShapeDtypeStruct((16, 16, 128), F32),
-        in_specs=[vmem] * 5,
+        in_specs=[pl.BlockSpec(memory_space=pltpu.HBM)] * 5,
         out_specs=vmem,
         scratch_shapes=scratch(shape),
         compiler_params=pltpu.CompilerParams(

time: 66.2 us -> 61.3 us (0.926)
  Pallas kernels: 61.3 us -> 56.2 us
    pallas_call x1, Pallas kernels: 61.3 us -> 56.2 us  [per_device(): pl.pallas_call(functools.partial(kernel, shape), out_shape=jax.ShapeDtype...]
where the time goes in v2:
time: 61.3 us; the launch traced here: 60.8 us
  Pallas kernels  56.2 us (92%)
  local copies, waits for them, and re-layouts  4.62 us (8%)
    pallas_call x1, Pallas kernels, per_device(): pl.pallas_call(functools.partial(kernel, shape), out_shape=jax.ShapeDtype...  56.2 us
    unnamed x11, local copies, waits for them, and re-layouts  4.62 us

profile of v2, /device:TPU:1, one launch (start us, length us, event | category | flops | bytes accessed | tf_op | source)
XLA Modules:
  0.0 60.8 jit_solution(13704943790159995249)
XLA Ops:
  0.0 0.0 copy-start.2
  0.0 0.7 %copy-done.2 = s32[1,1,1,1024,1]{3,4,2,1,0:T(1,128)S(1)} copy-done((s32[1,1,1,1024,1]{3,4,2,1,0:T(1,128)S(1)}, s32[1,1,1,1024,1]{3,4,2,1,0:T(1,128)}, u32[]{:S(2)}) %copy-start.2) | copy-done | bytes 4120
  0.7 0.0 copy-start
  0.7 1.0 %copy-done = f32[3,16,16,128]{3,2,1,0:T(8,128)S(1)} copy-done((f32[3,16,16,128]{3,2,1,0:T(8,128)S(1)}, f32[3,16,16,128]{3,2,1,0:T(8,128)}, u32[]{:S(2)}) %copy-start) | copy-done | bytes 393240
  1.7 0.0 copy-start.1
  1.7 0.9 %copy-done.1 = f32[16,16,128]{2,1,0:T(8,128)S(1)} copy-done((f32[16,16,128]{2,1,0:T(8,128)S(1)}, f32[16,16,128]{2,1,0:T(8,128)}, u32[]{:S(2)}) %copy-start.1) | copy-done | bytes 131096
  2.6 0.0 copy-start.3
  2.6 0.7 %copy-done.3 = s32[1,1,1,1024]{3,2,1,0:T(1,128)S(1)} copy-done((s32[1,1,1,1024]{3,2,1,0:T(1,128)S(1)}, s32[1,1,1,1024]{3,2,1,0:T(1,128)}, u32[]{:S(2)}) %copy-start.3) | copy-done | bytes 4120
  3.3 0.0 copy-start.4
  3.3 0.7 %copy-done.4 = f32[1,1,1,1024]{3,2,1,0:T(1,128)S(1)} copy-done((f32[1,1,1,1024]{3,2,1,0:T(1,128)S(1)}, f32[1,1,1,1024]{3,2,1,0:T(1,128)}, u32[]{:S(2)}) %copy-start.4) | copy-done | bytes 4120
  4.0 56.2 %cycle.1 = f32[16,16,128]{2,1,0:T(8,128)S(1)} custom-call(f32[16,16,128]{2,1,0:T(8,128)S(1)} %copy-done.1, f32[3,16,16,128]{3,2,1,0:T(8,128)S(1)} %copy-done, s32[8,128]{1,0:T(8,128)S(1)} %bitcast.3, s32[8,128]{1,0:T(8,128)S(1)} %bitcast.4, f32[8,128]{1,0:T(8,128)S(1)} %bitcast.5), custom_call_target="tpu_custom_call" | custom-call | tf_op jit(solution)/shard_map/cycle/pallas_call | solution.py:627
  60.2 0.7 %copy.7 = f32[16,16,128]{2,1,0:T(8,128)} copy(f32[16,16,128]{2,1,0:T(8,128)S(1)} %cycle.1) | data formatting | bytes 262144
Async XLA Ops:
  0.0 0.7 %copy-start.2 = (s32[1,1,1,1024,1]{3,4,2,1,0:T(1,128)S(1)}, s32[1,1,1,1024,1]{3,4,2,1,0:T(1,128)}, u32[]{:S(2)}) copy-start(s32[1,1,1,1024,1]{3,4,2,1,0:T(1,128)} %param.7) | copy-start | bytes 12292
  0.7 1.0 %copy-start = (f32[3,16,16,128]{3,2,1,0:T(8,128)S(1)}, f32[3,16,16,128]{3,2,1,0:T(8,128)}, u32[]{:S(2)}) copy-start(f32[3,16,16,128]{3,2,1,0:T(8,128)} %ind_hbm.1) | copy-start | bytes 1179652
  1.7 0.9 %copy-start.1 = (f32[16,16,128]{2,1,0:T(8,128)S(1)}, f32[16,16,128]{2,1,0:T(8,128)}, u32[]{:S(2)}) copy-start(f32[16,16,128]{2,1,0:T(8,128)} %chi_hbm.1) | copy-start | bytes 393220
  2.6 0.7 %copy-start.3 = (s32[1,1,1,1024]{3,2,1,0:T(1,128)S(1)}, s32[1,1,1,1024]{3,2,1,0:T(1,128)}, u32[]{:S(2)}) copy-start(s32[1,1,1,1024]{3,2,1,0:T(1,128)} %param.8) | copy-start | bytes 12292
  3.3 0.7 %copy-start.4 = (f32[1,1,1,1024]{3,2,1,0:T(1,128)S(1)}, f32[1,1,1,1024]{3,2,1,0:T(1,128)}, u32[]{:S(2)}) copy-start(f32[1,1,1,1024]{3,2,1,0:T(1,128)} %param.9) | copy-start | bytes 12292

commit v3 on v2

--- a/solution.py
+++ b/solution.py
@@ -16,6 +16,7 @@
 BOX.sort(key=lambda d: -sum(map(abs, d)))
 BOX2 = [d for d in itertools.product((-1, 0, 1), repeat=2) if d != (0, 0)]
 REACH = 5
+FAR = 15
 
 
 class Level:
@@ -106,8 +107,15 @@
 
     me = [lax.axis_index(a) for a in ("gx", "gy", "gz")]
 
+    known = {}
+
+    def along(i, o):
+        if (i, o) not in known:
+            known[i, o] = wrap(me[i] + o, shape[i]) if o else me[i]
+        return known[i, o]
+
     def device(o):
-        return tuple(lax.rem(me[i] + (o[i] + shape[i]), shape[i]) for i in range(3))
+        return tuple(along(i, o[i]) for i in range(3))
 
     barrier = pltpu.get_barrier_semaphore()
     all_peers = peers(shape)
@@ -162,6 +170,7 @@
     def ship_0(i, n):
         pack, land = pack_0.at[i], land_0.at[i]
         for d in BOX:
+            to = n + FAR if 0 not in d else n
             at, count = SLOT_0[d]
             if d[2] == 0:
                 if d[1] == 0:
@@ -170,25 +179,31 @@
                     first = (12 if d[1] == 1 else 20) + (6 if d[0] == 1 else 0)
             else:
                 first = (28 if d[2] == 1 else 30) + (1 if d[1] == 1 else 0)
-            send(pack.at[pl.ds(first, count)], land.at[pl.ds(at, count)], d, n)
-
-    def finish_0(dst, i, n):
+            send(pack.at[pl.ds(first, count)], land.at[pl.ds(at, count)], d, to)
+
+    def finish_0(dst, i, n, corners):
         land = land_0.at[i]
-        arrive(land, n)
+        if corners:
+            arrive(land.at[0:8], n + FAR)
+        else:
+            arrive(land.at[8:TILES_0], n)
         for xp in range(22):
             sx, px = (0, xp) if xp < 16 else (1, xp - 16) if xp < 19 else (-1, xp - 6)
             at = lambda y, z: SLOT_0[(-sx, -y, -z)][0]
             base = 6 if sx == -1 else 0
-            if sx:
+            if sx and not corners:
                 row = px - 13 if sx == -1 else px
                 dst[xp, 0:8, 0:128] = land[at(0, 0) + 2 * row]
                 dst[xp, 8:16, 0:128] = land[at(0, 0) + 2 * row + 1]
-            k = px // 2 - base
-            above, below = land[at(1, 0) + k], land[at(-1, 0) + k]
-            if px % 2:
-                above, below = pltpu.roll(above, 4, 0), pltpu.roll(below, 4, 0)
-            dst[xp, 16:24, 0:128] = jnp.where(sub < 4, above, below)
+            if not corners:
+                k = px // 2 - base
+                above, below = land[at(1, 0) + k], land[at(-1, 0) + k]
+                if px % 2:
+                    above, below = pltpu.roll(above, 4, 0), pltpu.roll(below, 4, 0)
+                dst[xp, 16:24, 0:128] = jnp.where(sub < 4, above, below)
             for t in range(3):
+                if corners != (sx != 0 and t == 2):
+                    continue
                 if t < 2:
                     a, b = land[at(0, 1) + t], land[at(0, -1) + t]
                 else:
@@ -213,39 +228,50 @@
             pack[4 + t] = up
             pack[6 + t] = down
         for d in BOX:
+            to = n + FAR if 0 not in d else n
             at, count = SLOT_1[d]
             if d[2] == 0:
                 first = 2 if d[0] == 1 else 0
             else:
                 first = (4 if d[2] == 1 else 6) + (1 if d[0] == 1 else 0)
-            send(pack.at[pl.ds(first, count)], land.at[pl.ds(at, count)], d, n)
-
-    def finish_1(dst, i, n):
+            send(pack.at[pl.ds(first, count)], land.at[pl.ds(at, count)], d, to)
+
+    def finish_1(dst, i, n, corners):
         land = land_1.at[i]
-        arrive(land, n)
+        if corners:
+            arrive(land.at[0:8], n + FAR)
+        else:
+            arrive(land.at[8:TILES_1], n)
         for xp in range(16):
             sx, px = (0, xp) if xp < 8 else (1, xp - 8) if xp < 12 else (-1, xp - 8)
             half = 1 if sx == -1 else 0
+            if corners and sx == 0:
+                continue
 
             def piece(y, z):
                 at = SLOT_1[(-sx, -y, -z)][0]
                 return land[at + px // 2 - 2 * half] if z == 0 else land[at + px // 4 - half]
 
-            for t in range(2):
-                if t == 0:
-                    a, b = piece(0, 1), piece(0, -1)
-                    if sx == 0:
-                        m = dst[xp, 0:8, :]
-                    else:
-                        m = piece(0, 0)
-                else:
-                    m, a, b = (jnp.where(sub < 4, piece(1, z), piece(-1, z)) for z in (0, 1, -1))
-                if px % 2 and not (t == 0 and sx == 0):
-                    m = pltpu.roll(m, 64, 1)
-                sa, sb = (64 - 32 * (px % 4)) % 128, 96 - 32 * (px % 4)
+            def both(z):
+                return jnp.where(sub < 4, piece(1, z), piece(-1, z))
+
+            sa, sb = (64 - 32 * (px % 4)) % 128, 96 - 32 * (px % 4)
+
+            def ends(a, b):
                 a = pltpu.roll(a, sa, 1) if sa else a
                 b = pltpu.roll(b, sb, 1) if sb else b
-                dst[xp, 8 * t : 8 * t + 8, :] = jnp.where(lane < 64, m, jnp.where(lane < 96, a, b))
+                return jnp.where(lane < 96, a, b)
+
+            def middle(m):
+                return pltpu.roll(m, 64, 1) if px % 2 else m
+
+            if corners:
+                dst[xp, 8:16, :] = jnp.where(lane < 64, dst[xp, 8:16, :], ends(both(1), both(-1)))
+                continue
+            m = middle(piece(0, 0)) if sx else dst[xp, 0:8, :]
+            dst[xp, 0:8, :] = jnp.where(lane < 64, m, ends(piece(0, 1), piece(0, -1)))
+            m = middle(both(0))
+            dst[xp, 8:16, :] = m if sx else jnp.where(lane < 64, m, ends(both(1), both(-1)))
 
     def start_2z(i, n):
         for k in (2, 1, 3):
@@ -442,8 +468,10 @@
 
     pl.semaphore_wait(barrier, len(all_peers))
 
-    for k in (2, 1, 3):
-        send(rec.at[0], rec.at[k], (0, 0, -k), 0)
+    rec_order = sorted(range(1, shape[2]), key=lambda k: min(k, shape[2] - k))
+    rec_sem = lambda k: (0, 33, 34)[k - 1]
+    for k in reversed(rec_order):
+        send(rec.at[0], rec.at[k], (0, 0, -k), rec_sem(k))
     FACES = [(1, 0, 0), (-1, 0, 0), (0, 1, 0), (0, -1, 0), (0, 0, 1), (0, 0, -1)]
     for j, d in enumerate(FACES):
         send(mom_out.at[j], mom_in.at[j], d, 1)
@@ -469,24 +497,19 @@
         row = jnp.where(to == mine, row, -1.0)
         parts = [p.astype(F32) for p in split3(rec[s, 16:24, :])]
         for j in range(8):
-            hot[:, 128 * j : 128 * j + 128] = jnp.where(rows256 == row[j : j + 1], 1.0, 0.0).astype(BF16)
+            hot[s % 2, :, 128 * j : 128 * j + 128] = jnp.where(rows256 == row[j : j + 1], 1.0, 0.0).astype(BF16)
             same = rows128 == col[j : j + 1]
             for q in range(3):
-                val_hot[128 * q : 128 * q + 128, 128 * j : 128 * j + 128] = jnp.where(same, parts[q][j : j + 1], 0.0).astype(BF16)
-        got = lax.dot_general(hot[...], val_hot[...], (((1,), (1,)), ((), ())), preferred_element_type=F32)
+                val_hot[s % 2, 128 * q : 128 * q + 128, 128 * j : 128 * j + 128] = jnp.where(same, parts[q][j : j + 1], 0.0).astype(BF16)
+        got = lax.dot_general(hot[s % 2], val_hot[s % 2], (((1,), (1,)), ((), ())), preferred_element_type=F32)
         return got[:, 0:128] + got[:, 128:256] + got[:, 256:384]
 
     rhs[...] = deposit(0)
-
-    arrive(rec.at[pl.ds(1, 3)], 0)
-
-    def more(s, carry):
-        rhs[...] = rhs[...] + deposit(s)
-        return carry
-
-    lax.fori_loop(1, shape[2], more, 0)
-
-    finish_0(K[0], 0, 2)
+    for k in rec_order:
+        arrive(rec.at[k], rec_sem(k))
+        rhs[...] = rhs[...] + deposit(k)
+
+    finish_0(K[0], 0, 2, False)
 
     arrive(mom_in, 1)
     inside = [
@@ -511,9 +534,11 @@
         B[0][x, 0:16, 0:128] = total * (OMEGA / sums)
     make_0(B[0], 1)
     ship_0(1, 5)
+    finish_0(K[0], 0, 2, True)
     coefficients(L0, 2)
 
-    finish_1(K[1], 0, 3)
+    finish_1(K[1], 0, 3, False)
+    finish_1(K[1], 0, 3, True)
     coefficients(L1, 3)
     start_2(finish_2z(0, 4), 0, 6)
     for p in range(4):
@@ -521,22 +546,26 @@
     restrict_2(lambda x: K[2][x, 0:8, :], 0)
     start_3y(0, 7)
 
-    finish_0(B[0], 1, 5)
-    sweep(L0, B[0], VA[0], 2)
+    finish_0(B[0], 1, 5, False)
+    sweep(L0, B[0], VA[0], 1)
 
     blocks = restrict_0(lambda x: residual(L0, VA[0], x)[0:16, 0:128])
     for p, block in enumerate(blocks):
         B[1][p, 0:8, :] = block * IW[1][p, 0:8, :]
     start_1(B[1], 1, 8)
+    finish_0(B[0], 1, 5, True)
+    sweep(L0, B[0], VA[0], 2)
     finish_2(K[2], 0, 6)
     coefficients(L2, 3)
     finish_3y(0, 7)
     start_3x(0, 9)
 
-    finish_1(B[1], 1, 8)
-    sweep(L1, B[1], VA[1], 3)
+    finish_1(B[1], 1, 8, False)
+    sweep(L1, B[1], VA[1], 1)
     restrict_1(lambda x: residual(L1, VA[1], x)[0:8, :], 1)
     start_2z(1, 10)
+    finish_1(B[1], 1, 8, True)
+    sweep(L1, B[1], VA[1], 3)
     finish_3x(K[3], 0, 9)
     coefficients(L3, 8)
 
@@ -582,12 +611,15 @@
         v, acc = gathered(L0, VB[0], x)
         out_ref[x] = ((1.0 - OMEGA) * v + acc)[0:16, 0:128]
 
-    sent(rec.at[pl.ds(1, 3)], 0)
+    for k in rec_order:
+        sent(rec.at[k], rec_sem(k))
     sent(mom_in, 1)
     for i, n in ((0, 2), (1, 5)):
-        sent(land_0.at[i], n)
+        sent(land_0.at[i, 8:TILES_0], n)
+        sent(land_0.at[i, 0:8], n + FAR)
     for i, n in ((0, 3), (1, 8)):
-        sent(land_1.at[i], n)
+        sent(land_1.at[i, 8:TILES_1], n)
+        sent(land_1.at[i, 0:8], n + FAR)
     for i, n in ((0, 4), (1, 10)):
         sent(land_2z.at[i], n)
     for i, n in ((0, 6), (1, 11), (2, 13)):
@@ -605,7 +637,7 @@
     nz = shape[2]
     out += [
         pltpu.VMEM((nz, 24, 128), F32), pltpu.VMEM((6, 16, 128), F32), pltpu.VMEM((6, 16, 128), F32),
-        pltpu.VMEM((256, 1024), BF16), pltpu.VMEM((384, 1024), BF16), pltpu.VMEM((256, 128), F32),
+        pltpu.VMEM((2, 256, 1024), BF16), pltpu.VMEM((2, 384, 1024), BF16), pltpu.VMEM((256, 128), F32),
         pltpu.VMEM((2, 32, 8, 128), F32), pltpu.VMEM((2, TILES_0, 8, 128), F32),
         pltpu.VMEM((2, 8, 8, 128), F32), pltpu.VMEM((2, TILES_1, 8, 128), F32),
         pltpu.VMEM((2, 16, 128), F32), pltpu.VMEM((2, nz - 1, 16, 128), F32),
@@ -617,7 +649,7 @@
         pltpu.VMEM((160, 128), F32),
         pltpu.VMEM((16, 16, 128), F32), pltpu.VMEM((3, 16, 16, 128), F32),
         pltpu.VMEM((2, 8, 128), jnp.int32), pltpu.VMEM((8, 128), F32),
-        pltpu.SemaphoreType.DMA((15,)), pltpu.SemaphoreType.DMA((15,)), pltpu.SemaphoreType.DMA((5,)),
+        pltpu.SemaphoreType.DMA((35,)), pltpu.SemaphoreType.DMA((35,)), pltpu.SemaphoreType.DMA((5,)),
     ]
     return out
 
@@ -631,7 +663,7 @@
         out_specs=vmem,
         scratch_shapes=scratch(shape),
         compiler_params=pltpu.CompilerParams(
-            collective_id=0, has_side_effects=True, vmem_limit_bytes=40 * 1024 * 1024
+            collective_id=0, has_side_effects=True, vmem_limit_bytes=60 * 1024 * 1024
         ),
         name="cycle",
     )(chi, inducing, record_dest.reshape(8, 128), record_cell.reshape(8, 128), record_value.reshape(8, 128))

time: 61.3 us -> 57.9 us (0.945)
  local copies, waits for them, and re-layouts: 4.62 us -> 1.57 us
    unnamed x11 -> x1, local copies, waits for them, and re-layouts: 4.62 us -> 1.57 us
where the time goes in v3:
time: 57.9 us; the launch traced here: 57.7 us
  Pallas kernels  56.1 us (97%)
  local copies, waits for them, and re-layouts  1.57 us (3%)
    pallas_call x1, Pallas kernels, per_device(): pl.pallas_call(functools.partial(kernel, shape), out_shape=jax.ShapeDtype...  56.1 us
    unnamed x1, local copies, waits for them, and re-layouts  1.57 us

profile of v3, /device:TPU:1, one launch (start us, length us, event | category | flops | bytes accessed | tf_op | source)
XLA Modules:
  0.0 57.7 jit_solution(4751688210744622899)
XLA Ops:
  0.0 56.1 %cycle.1 = f32[16,16,128]{2,1,0:T(8,128)} custom-call(f32[16,16,128]{2,1,0:T(8,128)} %chi_hbm.1, f32[3,16,16,128]{3,2,1,0:T(8,128)} %ind_hbm.1, s32[8,128]{1,0:T(8,128)} %bitcast.3, s32[8,128]{1,0:T(8,128)} %bitcast.4, f32[8,128]{1,0:T(8,128)} %bitcast.5), custom_call_target="tpu_custom_call" | custom-call | tf_op jit(solution)/shard_map/cycle/pallas_call | solution.py:659
  56.1 1.6 %copy.7 = f32[16,16,128]{2,1,0:T(8,128)} copy(f32[16,16,128]{2,1,0:T(8,128)} %cycle.1) | data formatting | bytes 262144

commit v4 on v3

--- a/solution.py
+++ b/solution.py
@@ -27,8 +27,8 @@
 
 L0 = Level(0, (16, 16, 128), (22, 24, 256), (19, 20, 192), (256, 192, 512))
 L1 = Level(1, (8, 8, 64), (16, 16, 128), (12, 12, 96), (128, 96, 256))
-L2 = Level(2, (4, 4, 0), (12, 16, 128), (8, 8, 128), (64, 48, 128))
-L3 = Level(3, (2, 2, 0), (22, 24, 128), (12, 24, 128), (32, 24, 64))
+L2 = Level(2, (4, 4, 32), (12, 16, 128), (8, 8, 128), (64, 48, 128))
+L3 = Level(3, (2, 2, 16), (22, 24, 128), (12, 24, 64), (32, 24, 64))
 LEVELS = (L0, L1, L2, L3)
 
 
@@ -61,7 +61,7 @@
 def peers(shape):
     nx, ny, nz = shape
     out = [tuple(d) for d in BOX]
-    out += [(0, 0, k) for k in range(2, nz - 1)]
+    out += [(x, y, k) for x in (-1, 0, 1) for y in (-1, 0, 1) for k in range(2, nz - 1)]
     out += [(0, k, 0) for k in range(-REACH, REACH + 1) if abs(k) > 1]
     out += [(k, 0, 0) for k in range(-REACH, REACH + 1) if abs(k) > 1]
     return out
@@ -133,6 +133,7 @@
 
     sub = lax.broadcasted_iota(jnp.int32, (8, 128), 0)
     lane = lax.broadcasted_iota(jnp.int32, (8, 128), 1)
+    lane24 = lax.broadcasted_iota(jnp.int32, (24, 128), 1)
     lane16 = lax.broadcasted_iota(jnp.int32, (16, 128), 1)
 
     def send(src, dst, o, n):
@@ -273,34 +274,48 @@
             m = middle(both(0))
             dst[xp, 8:16, :] = m if sx else jnp.where(lane < 64, m, ends(both(1), both(-1)))
 
+    columns = [(x, y, z) for x in (-1, 0, 1) for y in (-1, 0, 1) for z in range(shape[2]) if (x, y, z) != (0, 0, 0)]
+    columns.sort(key=lambda d: -(abs(d[0]) + abs(d[1]) + min(d[2], shape[2] - d[2])))
+
     def start_2z(i, n):
-        for k in (2, 1, 3):
-            send(pack_2.at[i], land_2z.at[i, k - 1], (0, 0, -k), n)
-
-    def finish_2z(i, n):
+        for j, d in enumerate(columns):
+            send(pack_2.at[i], land_2z.at[i, j], (d[0], d[1], -d[2]), n)
+
+    lane4 = lax.broadcasted_iota(jnp.int32, (4, 128), 1)
+
+    def pick(blocks):
+        out = blocks[3]
+        for g in (2, 1, 0):
+            out = jnp.where(lane4 < 32 * (g + 1), blocks[g], out)
+        return out
+
+    def finish_2z(dst, i, n):
         arrive(land_2z.at[i], n)
-        whole = pack_2[i]
-        for k in range(1, shape[2]):
-            whole = whole + land_2z[i, k - 1]
-        return whole
-
-    def start_2(whole, i, n):
-        full_2[i] = whole
+        for sx in (-1, 0, 1):
+            for sy in (-1, 0, 1):
+                own = [
+                    pack_2[i] if (sx, sy, z) == (0, 0, 0) else land_2z[i, columns.index((-sx, -sy, z))] for z in range(4)
+                ]
+                turned = []
+                for k in range(4):
+                    mixed = pick([own[(g + k) % 4] for g in range(4)])
+                    turned.append(pltpu.roll(mixed, 32 * k, 1) if k else mixed)
+                x0 = 0 if sx == 0 else 4 if sx == 1 else 8
+                y0 = 0 if sy == 0 else 4 if sy == 1 else 12
+                for p in range(4):
+                    dst[x0 + p, y0 : y0 + 4, :] = pick([turned[(z - p) % 4] for z in range(4)])
+
+    def start_2(n):
         for j, d in enumerate(BOX2):
-            send(full_2.at[i], land_2.at[i, j], (d[0], d[1], 0), n)
-
-    def place_2(dst, block, sx, sy):
-        x0 = 0 if sx == 0 else 4 if sx == 1 else 8
-        y0 = 0 if sy == 0 else 4 if sy == 1 else 12
-        for p in range(4):
-            dst[x0 + p, y0 : y0 + 4, :] = block[4 * p : 4 * p + 4, :]
-
-    def finish_2(dst, i, n, own=True):
-        arrive(land_2.at[i], n)
+            send(full_2, land_2.at[j], (d[0], d[1], 0), n)
+
+    def finish_2(dst, n):
+        arrive(land_2, n)
         for j, d in enumerate(BOX2):
-            place_2(dst, land_2[i, j], -d[0], -d[1])
-        if own:
-            place_2(dst, full_2[i], 0, 0)
+            x0 = 0 if d[0] == 0 else 4 if d[0] == -1 else 8
+            y0 = 0 if d[1] == 0 else 4 if d[1] == -1 else 12
+            for p in range(4):
+                dst[x0 + p, y0 : y0 + 4, :] = land_2[j, 4 * p : 4 * p + 4, :]
 
     steps = sorted([k for k in range(-REACH, REACH + 1) if k], key=lambda k: -abs(k))
 
@@ -324,8 +339,9 @@
         arrive(land_3x.at[i], n)
         for k in range(-REACH, REACH + 1):
             pair = col_3[i] if k == 0 else land_3x[i, steps.index(k)]
-            dst[(2 * k) % 22] = pair
-            dst[(2 * k + 1) % 22] = pltpu.roll(pair, 64, 1)
+            other = pltpu.roll(pair, 64, 1)
+            dst[(2 * k) % 22] = jnp.where(lane24 < 64, pair, other)
+            dst[(2 * k + 1) % 22] = jnp.where(lane24 < 64, other, pair)
 
     def around(ref, x, size):
         nx = size[0]
@@ -405,7 +421,7 @@
     down_rows_0 = eye((8, 16), lambda r, c: as_mat(half(c) == r))
     down_rows = eye((8, 8), lambda r, c: as_mat((half(c) == r) & (r < 4)))
     down_lanes_0 = eye((128, 128), lambda r, c: as_mat(half(r) == c, 0.125))
-    down_lanes_1 = eye((128, 128), lambda r, c: as_mat((half(r) + me[2] * 32 == c) & (r < 64), 0.125))
+    down_lanes_1 = eye((128, 128), lambda r, c: as_mat((half(r) == c) & (r < 64), 0.125))
     down_lanes_2 = [
         eye((128, 128), lambda r, c: as_mat(half(r) + 64 * p == c, 0.125)) for p in range(2)
     ]
@@ -416,12 +432,14 @@
         tall_0[...] = right(tall_0[...], down_lanes_0)
         return [left(down_rows_0, tall_0[16 * p : 16 * p + 16, :]) for p in range(8)]
 
-    def restrict_1(plane, i):
+    def restrict_1(plane):
         for p in range(4):
             tall_1[8 * p : 8 * p + 8, :] = plane(2 * p) + plane(2 * p + 1)
-        tall_1[...] = right(tall_1[...], down_lanes_1)
-        for p in range(4):
-            pack_2[i, 4 * p : 4 * p + 4, :] = left(down_rows, tall_1[8 * p : 8 * p + 8, :])[0:4]
+        part = right(tall_1[...], down_lanes_1)
+        whole = part[0:8]
+        for p in range(1, 4):
+            whole = whole + pltpu.roll(part[8 * p : 8 * p + 8], 32 * p, 1)
+        return left(down_rows, whole)[0:4]
 
     def restrict_2(plane, i):
         both = right(plane(0) + plane(1), down_lanes_2[0]) + right(plane(2) + plane(3), down_lanes_2[1])
@@ -483,7 +501,7 @@
     for p, block in enumerate(restrict_0(lambda x: K[0][x, 0:16, 0:128])):
         K[1][p, 0:8, :] = block
     start_1(K[1], 0, 3)
-    restrict_1(lambda x: K[1][x, 0:8, :], 0)
+    pack_2[0] = restrict_1(lambda x: K[1][x, 0:8, :])
     start_2z(0, 4)
 
     rows256 = lax.broadcasted_iota(jnp.int32, (256, 128), 0).astype(F32)
@@ -540,9 +558,7 @@
     finish_1(K[1], 0, 3, False)
     finish_1(K[1], 0, 3, True)
     coefficients(L1, 3)
-    start_2(finish_2z(0, 4), 0, 6)
-    for p in range(4):
-        K[2][p, 0:4, :] = full_2[0, 4 * p : 4 * p + 4, :]
+    finish_2z(K[2], 0, 4)
     restrict_2(lambda x: K[2][x, 0:8, :], 0)
     start_3y(0, 7)
 
@@ -555,40 +571,35 @@
     start_1(B[1], 1, 8)
     finish_0(B[0], 1, 5, True)
     sweep(L0, B[0], VA[0], 2)
-    finish_2(K[2], 0, 6)
     coefficients(L2, 3)
     finish_3y(0, 7)
     start_3x(0, 9)
 
     finish_1(B[1], 1, 8, False)
     sweep(L1, B[1], VA[1], 1)
-    restrict_1(lambda x: residual(L1, VA[1], x)[0:8, :], 1)
+    inv_2 = pick([pltpu.roll(IW[2][p, 0:4, :], 32 * p, 1) if p else IW[2][p, 0:4, :] for p in range(4)])
+    pack_2[1] = restrict_1(lambda x: residual(L1, VA[1], x)[0:8, :]) * inv_2
     start_2z(1, 10)
     finish_1(B[1], 1, 8, True)
     sweep(L1, B[1], VA[1], 3)
     finish_3x(K[3], 0, 9)
     coefficients(L3, 8)
 
-    whole = finish_2z(1, 10)
-    for p in range(4):
-        B[2][p, 0:4, :] = whole[4 * p : 4 * p + 4, :] * IW[2][p, 0:4, :]
-        full_2[1, 4 * p : 4 * p + 4, :] = B[2][p, 0:4, :]
-    start_2(full_2[1], 1, 11)
-    finish_2(B[2], 1, 11, own=False)
+    finish_2z(B[2], 1, 10)
     sweep(L2, B[2], VA[2], 3)
     restrict_2(lambda x: residual(L2, VA[2], x)[0:8, :], 1)
     own_rows = pack_3[1]
     low = IW[3][0, 0:2, :]
-    high = pltpu.roll(IW[3][1], 64, 1)[0:2, :]
+    high = IW[3][1, 0:2, :]
     pack_3[1] = own_rows * jnp.where(lax.broadcasted_iota(jnp.int32, (2, 128), 1) < 64, low, high)
     start_3y(1, 12)
     for p in range(4):
-        full_2[2, 4 * p : 4 * p + 4, :] = VA[2][p, 0:4, :]
-    start_2(full_2[2], 2, 13)
+        full_2[4 * p : 4 * p + 4, :] = VA[2][p, 0:4, :]
+    start_2(13)
 
     finish_3y(1, 12)
     start_3x(1, 14)
-    finish_2(VA[2], 2, 13, own=False)
+    finish_2(VA[2], 13)
     finish_3x(B[3], 1, 14)
     now, other = B[3], VA[3]
     for halo in range(8, 1, -1):
@@ -599,7 +610,7 @@
     prolong(L2, L3, 4, now, VA[2], tall_2, up_2, lambda r: wrap(half(jnp.where(r < 8, r, r - 16)), 24))
     sweep(L2, VA[2], VB[2], 3)
     sweep(L2, VB[2], VA[2], 2)
-    up_1 = eye((128, 128), lambda r, c: as_mat(r == wrap(half(jnp.where(c < 96, c, c - 128)) + 32 * me[2], 128)))
+    up_1 = eye((128, 128), lambda r, c: as_mat(r == wrap(half(jnp.where(c < 96, c, c - 128)), 128)))
     prolong(L1, L2, 3, VA[2], VA[1], tall_3, up_1, lambda r: wrap(half(jnp.where(r < 12, r, r - 16)), 16))
     sweep(L1, VA[1], VB[1], 2)
     sweep(L1, VB[1], VA[1], 1)
@@ -622,8 +633,7 @@
         sent(land_1.at[i, 0:8], n + FAR)
     for i, n in ((0, 4), (1, 10)):
         sent(land_2z.at[i], n)
-    for i, n in ((0, 6), (1, 11), (2, 13)):
-        sent(land_2.at[i], n)
+    sent(land_2, 13)
     for i, n in ((0, 7), (1, 12)):
         sent(land_3y.at[i], n)
     for i, n in ((0, 9), (1, 14)):
@@ -640,8 +650,8 @@
         pltpu.VMEM((2, 256, 1024), BF16), pltpu.VMEM((2, 384, 1024), BF16), pltpu.VMEM((256, 128), F32),
         pltpu.VMEM((2, 32, 8, 128), F32), pltpu.VMEM((2, TILES_0, 8, 128), F32),
         pltpu.VMEM((2, 8, 8, 128), F32), pltpu.VMEM((2, TILES_1, 8, 128), F32),
-        pltpu.VMEM((2, 16, 128), F32), pltpu.VMEM((2, nz - 1, 16, 128), F32),
-        pltpu.VMEM((3, 16, 128), F32), pltpu.VMEM((3, 8, 16, 128), F32),
+        pltpu.VMEM((2, 4, 128), F32), pltpu.VMEM((2, 9 * nz - 1, 4, 128), F32),
+        pltpu.VMEM((16, 128), F32), pltpu.VMEM((8, 16, 128), F32),
         pltpu.VMEM((2, 2, 128), F32), pltpu.VMEM((2, 2 * REACH, 2, 128), F32),
         pltpu.VMEM((2, 24, 128), F32), pltpu.VMEM((2, 2 * REACH, 24, 128), F32),
         pltpu.VMEM((128, 128), F32), pltpu.VMEM((32, 128), F32),
@@ -656,6 +666,7 @@
 
 def per_device(shape, chi, inducing, record_dest, record_cell, record_value):
     vmem = pl.BlockSpec(memory_space=pltpu.VMEM)
+    keep = lambda a: pltpu.with_memory_space_constraint(a, pltpu.HBM)
     return pl.pallas_call(
         functools.partial(kernel, shape),
         out_shape=jax.ShapeDtypeStruct((16, 16, 128), F32),
@@ -663,10 +674,10 @@
         out_specs=vmem,
         scratch_shapes=scratch(shape),
         compiler_params=pltpu.CompilerParams(
-            collective_id=0, has_side_effects=True, vmem_limit_bytes=60 * 1024 * 1024
+            collective_id=0, has_side_effects=True, vmem_limit_bytes=40 * 1024 * 1024
         ),
         name="cycle",
-    )(chi, inducing, record_dest.reshape(8, 128), record_cell.reshape(8, 128), record_value.reshape(8, 128))
+    )(*map(keep, (chi, inducing, record_dest.reshape(8, 128), record_cell.reshape(8, 128), record_value.reshape(8, 128))))
 
 
 def solution(mesh):

time: 57.9 us -> 54.2 us (0.936)
  Pallas kernels: 56.1 us -> 53.3 us
  local copies, waits for them, and re-layouts: 1.57 us -> 0.66 us
    pallas_call x1, Pallas kernels: 56.1 us -> 53.3 us  [per_device(): pl.pallas_call(functools.partial(kernel, shape), out_shape=jax.ShapeDtype...]
    unnamed x1, local copies, waits for them, and re-layouts: 1.57 us -> 0.66 us
where the time goes in v4:
time: 54.2 us; the launch traced here: 53.9 us
  Pallas kernels  53.3 us (98%)
  local copies, waits for them, and re-layouts  0.66 us (1%)
    pallas_call x1, Pallas kernels, per_device(): pl.pallas_call(functools.partial(kernel, shape), out_shape=jax.ShapeDtype...  53.3 us

profile of v4, /device:TPU:1, one launch (start us, length us, event | category | flops | bytes accessed | tf_op | source)
XLA Modules:
  0.0 53.9 jit_solution(12665210881508205821)
XLA Ops:
  0.0 53.3 %cycle.1 = f32[16,16,128]{2,1,0:T(8,128)S(1)} custom-call(f32[16,16,128]{2,1,0:T(8,128)} %chi_hbm.1, f32[3,16,16,128]{3,2,1,0:T(8,128)} %ind_hbm.1, s32[8,128]{1,0:T(8,128)} %bitcast.3, s32[8,128]{1,0:T(8,128)} %bitcast.4, f32[8,128]{1,0:T(8,128)} %bitcast.5), custom_call_target="tpu_custom_call" | custom-call | tf_op jit(solution)/shard_map/cycle/pallas_call | solution.py:670
  53.3 0.7 %copy.7 = f32[16,16,128]{2,1,0:T(8,128)} copy(f32[16,16,128]{2,1,0:T(8,128)S(1)} %cycle.1) | data formatting | bytes 262144

commit v5 on v4

--- a/solution.py
+++ b/solution.py
@@ -117,11 +117,6 @@
     def device(o):
         return tuple(along(i, o[i]) for i in range(3))
 
-    barrier = pltpu.get_barrier_semaphore()
-    all_peers = peers(shape)
-    for o in all_peers:
-        pl.semaphore_signal(barrier, inc=1, device_id=device(o), device_id_type=MESH)
-
     copies = [
         pltpu.make_async_copy(src, dst, load_sem.at[j])
         for j, (src, dst) in enumerate([
@@ -130,6 +125,11 @@
     ]
     for j in (2, 3, 4, 0, 1):
         copies[j].start()
+
+    barrier = pltpu.get_barrier_semaphore()
+    all_peers = peers(shape)
+    for o in all_peers:
+        pl.semaphore_signal(barrier, inc=1, device_id=device(o), device_id_type=MESH)
 
     sub = lax.broadcasted_iota(jnp.int32, (8, 128), 0)
     lane = lax.broadcasted_iota(jnp.int32, (8, 128), 1)
@@ -418,8 +418,6 @@
         return jnp.where(cond, value, 0.0).astype(BF16)
 
     half = lambda a: lax.shift_right_arithmetic(a, 1)
-    down_rows_0 = eye((8, 16), lambda r, c: as_mat(half(c) == r))
-    down_rows = eye((8, 8), lambda r, c: as_mat((half(c) == r) & (r < 4)))
     down_lanes_0 = eye((128, 128), lambda r, c: as_mat(half(r) == c, 0.125))
     down_lanes_1 = eye((128, 128), lambda r, c: as_mat((half(r) == c) & (r < 64), 0.125))
     down_lanes_2 = [
@@ -429,21 +427,22 @@
     def restrict_0(plane):
         for p in range(8):
             tall_0[16 * p : 16 * p + 16, :] = plane(2 * p) + plane(2 * p + 1)
-        tall_0[...] = right(tall_0[...], down_lanes_0)
-        return [left(down_rows_0, tall_0[16 * p : 16 * p + 16, :]) for p in range(8)]
+        rows = right(tall_0[pl.ds(0, 64, 2), :] + tall_0[pl.ds(1, 64, 2), :], down_lanes_0)
+        return [rows[8 * p : 8 * p + 8] for p in range(8)]
 
     def restrict_1(plane):
         for p in range(4):
             tall_1[8 * p : 8 * p + 8, :] = plane(2 * p) + plane(2 * p + 1)
-        part = right(tall_1[...], down_lanes_1)
-        whole = part[0:8]
+        part = right(tall_1[pl.ds(0, 16, 2), :] + tall_1[pl.ds(1, 16, 2), :], down_lanes_1)
+        whole = part[0:4]
         for p in range(1, 4):
-            whole = whole + pltpu.roll(part[8 * p : 8 * p + 8], 32 * p, 1)
-        return left(down_rows, whole)[0:4]
+            whole = whole + pltpu.roll(part[4 * p : 4 * p + 4], 32 * p, 1)
+        return whole
 
     def restrict_2(plane, i):
         both = right(plane(0) + plane(1), down_lanes_2[0]) + right(plane(2) + plane(3), down_lanes_2[1])
-        pack_3[i] = left(down_rows, both)[0:2]
+        for r in range(2):
+            pack_3[i, r : r + 1, :] = both[2 * r : 2 * r + 1] + both[2 * r + 1 : 2 * r + 2]
 
     def prolong(fine, coarse, halo, e_ref, v_ref, tall, lanes_mat, rows_of):
         XF, YF, ZF = fine.size
@@ -465,6 +464,12 @@
     rec[0, 0:8, :] = rec_in[0].astype(F32)
     rec[0, 8:16, :] = rec_in[1].astype(F32)
     rec[0, 16:24, :] = val_in[...]
+    pl.semaphore_wait(barrier, len(all_peers))
+
+    rec_order = sorted(range(1, shape[2]), key=lambda k: min(k, shape[2] - k))
+    rec_sem = lambda k: (0, 33, 34)[k - 1]
+    for k in reversed(rec_order):
+        send(rec.at[0], rec.at[k], (0, 0, -k), rec_sem(k))
     copies[0].wait()
     for x in range(16):
         K[0][x, 0:16, 0:128] = 1.0 + chi[x]
@@ -484,12 +489,6 @@
     mom_out[4] = up
     mom_out[5] = down
 
-    pl.semaphore_wait(barrier, len(all_peers))
-
-    rec_order = sorted(range(1, shape[2]), key=lambda k: min(k, shape[2] - k))
-    rec_sem = lambda k: (0, 33, 34)[k - 1]
-    for k in reversed(rec_order):
-        send(rec.at[0], rec.at[k], (0, 0, -k), rec_sem(k))
     FACES = [(1, 0, 0), (-1, 0, 0), (0, 1, 0), (0, -1, 0), (0, 0, 1), (0, 0, -1)]
     for j, d in enumerate(FACES):
         send(mom_out.at[j], mom_in.at[j], d, 1)
@@ -522,7 +521,18 @@
         got = lax.dot_general(hot[s % 2], val_hot[s % 2], (((1,), (1,)), ((), ())), preferred_element_type=F32)
         return got[:, 0:128] + got[:, 128:256] + got[:, 256:384]
 
-    rhs[...] = deposit(0)
+    row16 = lax.broadcasted_iota(jnp.int32, (16, 128), 0)
+    for x in range(16):
+        my = chi[x] * ind[1, x]
+        mz = chi[x] * ind[2, x]
+        inner = jnp.where(row16 == 15, 0.0, pltpu.roll(my, 15, 0)) - jnp.where(row16 == 0, 0.0, pltpu.roll(my, 1, 0))
+        inner = inner + jnp.where(lane16 == 127, 0.0, pltpu.roll(mz, 127, 1)) - jnp.where(lane16 == 0, 0.0, pltpu.roll(mz, 1, 1))
+        if x < 15:
+            inner = inner + chi[x + 1] * ind[0, x + 1]
+        if x > 0:
+            inner = inner - chi[x - 1] * ind[0, x - 1]
+        rhs[16 * x : 16 * x + 16, :] = -0.5 * inner
+    rhs[...] = rhs[...] + deposit(0)
     for k in rec_order:
         arrive(rec.at[k], rec_sem(k))
         rhs[...] = rhs[...] + deposit(k)
@@ -534,20 +544,20 @@
         jnp.where(me[i] == edge, 0.0, 1.0) for i in range(3) for edge in (shape[i] - 1, 0)
     ]
     masks_0 = edge_masks(L0)
-    row16 = lax.broadcasted_iota(jnp.int32, (16, 128), 0)
+    mom_in[0] = mom_in[0] * inside[1]
+    mom_in[1] = mom_in[1] * inside[0]
+    far_all = mom_in[5] * inside[4]
+    near_all = mom_in[4] * inside[5]
     for x in range(16):
-        xp = chi[x + 1] * ind[0, x + 1] if x < 15 else mom_in[1] * inside[0]
-        xm = chi[x - 1] * ind[0, x - 1] if x > 0 else mom_in[0] * inside[1]
-        my = chi[x] * ind[1, x]
-        yp = jnp.where(row16 == 15, mom_in[3, x : x + 1, :] * inside[2], pltpu.roll(my, 15, 0))
-        ym = jnp.where(row16 == 0, mom_in[2, x : x + 1, :] * inside[3], pltpu.roll(my, 1, 0))
-        mz = chi[x] * ind[2, x]
-        far = pltpu.roll(mom_in[5] * inside[4], 127 - x, 1)
-        near = mom_in[4] * inside[5]
-        near = pltpu.roll(near, 128 - x, 1) if x else near
-        zp = jnp.where(lane16 == 127, far, pltpu.roll(mz, 127, 1))
-        zm = jnp.where(lane16 == 0, near, pltpu.roll(mz, 1, 1))
-        total = -0.5 * (xp - xm + (yp - ym) + (zp - zm)) + rhs[16 * x : 16 * x + 16, :]
+        edge = jnp.where(row16 == 15, mom_in[3, x : x + 1, :] * inside[2], 0.0)
+        edge = edge - jnp.where(row16 == 0, mom_in[2, x : x + 1, :] * inside[3], 0.0)
+        near = pltpu.roll(near_all, 128 - x, 1) if x else near_all
+        edge = edge + jnp.where(lane16 == 127, pltpu.roll(far_all, 127 - x, 1), 0.0) - jnp.where(lane16 == 0, near, 0.0)
+        if x == 15:
+            edge = edge + mom_in[1]
+        if x == 0:
+            edge = edge - mom_in[0]
+        total = rhs[16 * x : 16 * x + 16, :] - 0.5 * edge
         sums = face_sums(L0, x, masks_0(x))[1][0:16, 0:128]
         B[0][x, 0:16, 0:128] = total * (OMEGA / sums)
     make_0(B[0], 1)

time: 54.2 us -> 54 us (level)
  no operation moved by 1% of the time
where the time goes in v5:
time: 54 us; the launch traced here: 53.8 us
  Pallas kernels  53.2 us (99%)
  local copies, waits for them, and re-layouts  0.66 us (1%)
    pallas_call x1, Pallas kernels, per_device(): pl.pallas_call(functools.partial(kernel, shape), out_shape=jax.ShapeDtype...  53.2 us

profile of v5, /device:TPU:1, one launch (start us, length us, event | category | flops | bytes accessed | tf_op | source)
XLA Modules:
  0.0 53.8 jit_solution(11812812059122586951)
XLA Ops:
  0.0 53.2 %cycle.1 = f32[16,16,128]{2,1,0:T(8,128)S(1)} custom-call(f32[16,16,128]{2,1,0:T(8,128)} %chi_hbm.1, f32[3,16,16,128]{3,2,1,0:T(8,128)} %ind_hbm.1, s32[8,128]{1,0:T(8,128)} %bitcast.3, s32[8,128]{1,0:T(8,128)} %bitcast.4, f32[8,128]{1,0:T(8,128)} %bitcast.5), custom_call_target="tpu_custom_call" | custom-call | tf_op jit(solution)/shard_map/cycle/pallas_call | solution.py:680
  53.2 0.7 %copy.7 = f32[16,16,128]{2,1,0:T(8,128)} copy(f32[16,16,128]{2,1,0:T(8,128)S(1)} %cycle.1) | data formatting | bytes 262144

commit v6 on v5

--- a/solution.py
+++ b/solution.py
@@ -19,6 +19,19 @@
 FAR = 15
 
 
+def apart(k):
+    return max(0, 2 * abs(k) - 3)
+
+
+DIAMOND = [
+    (a, b)
+    for a in range(-REACH, REACH + 1)
+    for b in range(-REACH, REACH + 1)
+    if (a, b) != (0, 0) and apart(a) + apart(b) <= apart(REACH)
+]
+DIAMOND.sort(key=lambda d: -(abs(d[1]) + abs(d[0]) / 2))
+
+
 class Level:
     def __init__(self, index, own, size, split, total):
         self.index, self.own, self.size, self.split, self.total = index, own, size, split, total
@@ -62,8 +75,7 @@
     nx, ny, nz = shape
     out = [tuple(d) for d in BOX]
     out += [(x, y, k) for x in (-1, 0, 1) for y in (-1, 0, 1) for k in range(2, nz - 1)]
-    out += [(0, k, 0) for k in range(-REACH, REACH + 1) if abs(k) > 1]
-    out += [(k, 0, 0) for k in range(-REACH, REACH + 1) if abs(k) > 1]
+    out += [(a, b, 0) for a, b in reversed(DIAMOND) if max(abs(a), abs(b)) > 1]
     return out
 
 
@@ -100,7 +112,7 @@
     rec, mom_out, mom_in, hot, val_hot, rhs = take(6)
     pack_0, land_0, pack_1, land_1 = take(4)
     pack_2, land_2z, full_2, land_2 = take(4)
-    pack_3, land_3y, col_3, land_3x = take(4)
+    pack_3, land_3, col_3 = take(3)
     tall_0, tall_1, tall_2, tall_3, tall_4 = take(5)
     chi, ind, rec_in, val_in = take(4)
     send_sem, recv_sem, load_sem = take(3)
@@ -317,28 +329,21 @@
             for p in range(4):
                 dst[x0 + p, y0 : y0 + 4, :] = land_2[j, 4 * p : 4 * p + 4, :]
 
-    steps = sorted([k for k in range(-REACH, REACH + 1) if k], key=lambda k: -abs(k))
-
-    def start_3y(i, n):
-        for j, k in enumerate(steps):
-            send(pack_3.at[i], land_3y.at[i, j], (0, -k, 0), n)
-
-    def finish_3y(i, n):
-        arrive(land_3y.at[i], n)
-        col_3[i, 2 * REACH + 2 : 24 - 2 * REACH, :] = jnp.zeros((22 - 4 * REACH, 128), F32)
-        col_3[i, 0:2, :] = pack_3[i]
-        for j, k in enumerate(steps):
-            row = (2 * k) % 24
-            col_3[i, row : row + 2, :] = land_3y[i, j]
-
-    def start_3x(i, n):
-        for j, k in enumerate(steps):
-            send(col_3.at[i], land_3x.at[i, j], (-k, 0, 0), n)
-
-    def finish_3x(dst, i, n):
-        arrive(land_3x.at[i], n)
+    def start_3(i, n):
+        for j, d in enumerate(DIAMOND):
+            send(pack_3.at[i], land_3.at[i, j], (d[0], d[1], 0), n)
+
+    def finish_3(dst, i, n):
+        arrive(land_3.at[i], n)
+        for a in range(-REACH, REACH + 1):
+            for b in range(-REACH, REACH + 1):
+                row = (2 * b) % 24
+                if (a, b) == (0, 0):
+                    col_3[i, REACH, 0:2, :] = pack_3[i]
+                elif (-a, -b) in DIAMOND:
+                    col_3[i, a + REACH, row : row + 2, :] = land_3[i, DIAMOND.index((-a, -b))]
         for k in range(-REACH, REACH + 1):
-            pair = col_3[i] if k == 0 else land_3x[i, steps.index(k)]
+            pair = col_3[i, k + REACH]
             other = pltpu.roll(pair, 64, 1)
             dst[(2 * k) % 22] = jnp.where(lane24 < 64, pair, other)
             dst[(2 * k + 1) % 22] = jnp.where(lane24 < 64, other, pair)
@@ -494,6 +499,9 @@
         send(mom_out.at[j], mom_in.at[j], d, 1)
     ship_0(0, 2)
 
+    for k in range(2 * REACH + 1):
+        for i in range(2):
+            col_3[i, k] = jnp.zeros((24, 128), F32)
     for ref in (K[2], B[2]):
         for x in range(12):
             ref[x, 8:16, :] = jnp.zeros((8, 128), F32)
@@ -570,7 +578,6 @@
     coefficients(L1, 3)
     finish_2z(K[2], 0, 4)
     restrict_2(lambda x: K[2][x, 0:8, :], 0)
-    start_3y(0, 7)
 
     finish_0(B[0], 1, 5, False)
     sweep(L0, B[0], VA[0], 1)
@@ -579,11 +586,10 @@
     for p, block in enumerate(blocks):
         B[1][p, 0:8, :] = block * IW[1][p, 0:8, :]
     start_1(B[1], 1, 8)
+    start_3(0, 7)
     finish_0(B[0], 1, 5, True)
     sweep(L0, B[0], VA[0], 2)
     coefficients(L2, 3)
-    finish_3y(0, 7)
-    start_3x(0, 9)
 
     finish_1(B[1], 1, 8, False)
     sweep(L1, B[1], VA[1], 1)
@@ -592,7 +598,7 @@
     start_2z(1, 10)
     finish_1(B[1], 1, 8, True)
     sweep(L1, B[1], VA[1], 3)
-    finish_3x(K[3], 0, 9)
+    finish_3(K[3], 0, 7)
     coefficients(L3, 8)
 
     finish_2z(B[2], 1, 10)
@@ -602,15 +608,13 @@
     low = IW[3][0, 0:2, :]
     high = IW[3][1, 0:2, :]
     pack_3[1] = own_rows * jnp.where(lax.broadcasted_iota(jnp.int32, (2, 128), 1) < 64, low, high)
-    start_3y(1, 12)
+    start_3(1, 12)
     for p in range(4):
         full_2[4 * p : 4 * p + 4, :] = VA[2][p, 0:4, :]
     start_2(13)
 
-    finish_3y(1, 12)
-    start_3x(1, 14)
     finish_2(VA[2], 13)
-    finish_3x(B[3], 1, 14)
+    finish_3(B[3], 1, 12)
     now, other = B[3], VA[3]
     for halo in range(8, 1, -1):
         sweep(L3, now, other, halo)
@@ -645,9 +649,7 @@
         sent(land_2z.at[i], n)
     sent(land_2, 13)
     for i, n in ((0, 7), (1, 12)):
-        sent(land_3y.at[i], n)
-    for i, n in ((0, 9), (1, 14)):
-        sent(land_3x.at[i], n)
+        sent(land_3.at[i], n)
 
 
 def scratch(shape):
@@ -662,8 +664,8 @@
         pltpu.VMEM((2, 8, 8, 128), F32), pltpu.VMEM((2, TILES_1, 8, 128), F32),
         pltpu.VMEM((2, 4, 128), F32), pltpu.VMEM((2, 9 * nz - 1, 4, 128), F32),
         pltpu.VMEM((16, 128), F32), pltpu.VMEM((8, 16, 128), F32),
-        pltpu.VMEM((2, 2, 128), F32), pltpu.VMEM((2, 2 * REACH, 2, 128), F32),
-        pltpu.VMEM((2, 24, 128), F32), pltpu.VMEM((2, 2 * REACH, 24, 128), F32),
+        pltpu.VMEM((2, 2, 128), F32), pltpu.VMEM((2, len(DIAMOND), 2, 128), F32),
+        pltpu.VMEM((2, 2 * REACH + 1, 24, 128), F32),
         pltpu.VMEM((128, 128), F32), pltpu.VMEM((32, 128), F32),
         pltpu.VMEM((144, 128), F32), pltpu.VMEM((128, 128), F32),
         pltpu.VMEM((160, 128), F32),

time: 54 us -> 52.4 us (0.970)
  Pallas kernels: 53.2 us -> 51.7 us
    pallas_call x1, Pallas kernels: 53.2 us -> 51.7 us  [per_device(): pl.pallas_call(functools.partial(kernel, shape), out_shape=jax.ShapeDtype...]
where the time goes in v6:
time: 52.4 us; the launch traced here: 52.3 us
  Pallas kernels  51.7 us (99%)
  local copies, waits for them, and re-layouts  0.66 us (1%)
    pallas_call x1, Pallas kernels, per_device(): pl.pallas_call(functools.partial(kernel, shape), out_shape=jax.ShapeDtype...  51.7 us

profile of v6, /device:TPU:1, one launch (start us, length us, event | category | flops | bytes accessed | tf_op | source)
XLA Modules:
  0.0 52.3 jit_solution(4345917876696194804)
XLA Ops:
  0.0 51.7 %cycle.1 = f32[16,16,128]{2,1,0:T(8,128)S(1)} custom-call(f32[16,16,128]{2,1,0:T(8,128)} %chi_hbm.1, f32[3,16,16,128]{3,2,1,0:T(8,128)} %ind_hbm.1, s32[8,128]{1,0:T(8,128)} %bitcast.3, s32[8,128]{1,0:T(8,128)} %bitcast.4, f32[8,128]{1,0:T(8,128)} %bitcast.5), custom_call_target="tpu_custom_call" | custom-call | tf_op jit(solution)/shard_map/cycle/pallas_call | solution.py:682
  51.7 0.7 %copy.7 = f32[16,16,128]{2,1,0:T(8,128)} copy(f32[16,16,128]{2,1,0:T(8,128)S(1)} %cycle.1) | data formatting | bytes 262144
